TPU v7x, 128 devices: a whole 4x4x4 slice. The times are simulated.
128 devices in a mesh: dp: 64 (over y_hi, z, x, core), col: 2 (over y_lo).
Axes of the slice: x: 4, y: 4 (y_hi: 2, y_lo: 2; y = y_hi * 2 + y_lo), z: 4, core: 2. Of those that a mesh axis runs over, the one named last changes fastest.
Arguments:
- tokens: bfloat16 [8192, 2048], P('dp'), may hold values from -6 to 6
- routes: int32 [8192, 8], P('dp'), may hold values from 0 to 127, all different within a row; in each aligned block of 128 rows (0 to 127, 128 to 255, ...) at most 12 rows name the same one
- probs: float32 [8192, 8], P('dp'), may hold values from 0.1 to 1
- w_gate: bfloat16 [128, 2048, 768], P('dp', None, 'col'), may hold values from -0.125 to 0.125
- w_up: bfloat16 [128, 2048, 768], P('dp', None, 'col'), may hold values from -0.125 to 0.125
- w_down: bfloat16 [128, 768, 2048], P('dp', 'col'), may hold values from -0.21875 to 0.21875
- cotangent: bfloat16 [8192, 2048], P('dp', 'col'), may hold values from -6 to 6
Outputs:
- mixed: bfloat16 [8192, 2048], P('dp', 'col')
- grad_tokens: bfloat16 [8192, 2048], P('dp', 'col')
- grad_probs: float32 [8192, 8], P('dp')
- grad_gate: bfloat16 [128, 2048, 768], P('dp', None, 'col')
- grad_up: bfloat16 [128, 2048, 768], P('dp', None, 'col')
- grad_down: bfloat16 [128, 768, 2048], P('dp', 'col')
Inputs may be any that keep to these rules, and one draw needn't show every extreme that they name: `routes`: each token names 8 different experts. Among the 128 tokens of one index of dp, no expert is named by more than 12 of them, a bound that some block reaches.
All inputs are finite; a program needn't handle non-finite values.
Results may differ from a plain program's by a relative error of at most 0.0064.
Values may be sent and summed in bfloat16 or wider, within the bound.
A program may use at most 192 MiB of HBM per device.

v0:
```python
import jax
import jax.numpy as jnp
from jax import lax
from jax.sharding import PartitionSpec as P


def body(tokens, routes, probs, w_gate, w_up, w_down, cotangent):
    tok_count, width = tokens.shape
    top_count = routes.shape[1]
    owners = lax.axis_size("dp")
    local_experts = w_gate.shape[0]
    experts = local_experts * owners
    slot_cap = 3 * tok_count * top_count // (2 * experts)
    half_width = width // lax.axis_size("col")
    flat_routes = routes.reshape(-1)
    expert_ids = jnp.arange(experts, dtype=jnp.int32)
    onehot = (flat_routes[:, None] == expert_ids[None, :]).astype(jnp.int32)
    before = jnp.cumsum(onehot, axis=0) - onehot
    slot_index = jnp.sum(before * onehot, axis=1)
    flat_index = flat_routes * slot_cap + slot_index

    def scatter_rows(row_pairs):
        buffer = jnp.zeros((experts * slot_cap, row_pairs.shape[1]), row_pairs.dtype)
        buffer = buffer.at[flat_index].set(row_pairs)
        return buffer.reshape(owners, local_experts * slot_cap, row_pairs.shape[1])

    def send_whole(row_pairs):
        return lax.all_to_all(
            scatter_rows(row_pairs), "dp", split_axis=0, concat_axis=0, tiled=True
        )

    def send_back(partial_value):
        summed = lax.psum_scatter(partial_value, "col", scatter_dimension=2, tiled=True).astype(
            jnp.bfloat16
        )
        returned = lax.all_to_all(summed, "dp", split_axis=0, concat_axis=0, tiled=True)
        return returned.reshape(experts * slot_cap, half_width)[flat_index].reshape(
            tok_count, top_count, half_width
        )

    arrived_rows = send_whole(jnp.repeat(tokens, top_count, axis=0))
    row_block = arrived_rows.reshape(owners, local_experts, slot_cap, width)
    gate_acts = jnp.einsum("slcd,ldh->slch", row_block, w_gate, preferred_element_type=jnp.float32)
    up_acts = jnp.einsum("slcd,ldh->slch", row_block, w_up, preferred_element_type=jnp.float32)
    sigmoid_g = jax.nn.sigmoid(gate_acts)
    silu_g = gate_acts * sigmoid_g
    hidden = (silu_g * up_acts).astype(jnp.bfloat16)
    out_partial = jnp.einsum("slch,lhd->slcd", hidden, w_down, preferred_element_type=jnp.float32)
    picked_out = send_back(out_partial.reshape(owners, local_experts * slot_cap, width))
    picked_wide = picked_out.astype(jnp.float32)
    mixed = jnp.sum(probs[:, :, None] * picked_wide, axis=1).astype(jnp.bfloat16)
    cot_wide = cotangent.astype(jnp.float32)
    prob_part = jnp.sum(cot_wide[:, None, :] * picked_wide, axis=2)
    full_cot = lax.all_gather(cotangent, "col", axis=1, tiled=True)
    scaled_full = (probs[:, :, None] * full_cot.astype(jnp.float32)[:, None, :]).astype(
        jnp.bfloat16
    )
    arrived_cot = send_whole(scaled_full.reshape(tok_count * top_count, width))
    d_out = arrived_cot.reshape(owners, local_experts, slot_cap, width)
    grad_down = jnp.einsum(
        "slch,slcd->lhd", hidden, d_out, preferred_element_type=jnp.float32
    ).astype(jnp.bfloat16)
    d_hidden = jnp.einsum("slcd,lhd->slch", d_out, w_down, preferred_element_type=jnp.float32)
    d_gate = (d_hidden * up_acts * sigmoid_g * (1.0 + gate_acts * (1.0 - sigmoid_g))).astype(
        jnp.bfloat16
    )
    d_up = (d_hidden * silu_g).astype(jnp.bfloat16)
    grad_gate = jnp.einsum(
        "slcd,slch->ldh", row_block, d_gate, preferred_element_type=jnp.float32
    ).astype(jnp.bfloat16)
    grad_up = jnp.einsum(
        "slcd,slch->ldh", row_block, d_up, preferred_element_type=jnp.float32
    ).astype(jnp.bfloat16)
    d_partial = jnp.einsum(
        "slch,ldh->slcd", d_gate, w_gate, preferred_element_type=jnp.float32
    ) + jnp.einsum("slch,ldh->slcd", d_up, w_up, preferred_element_type=jnp.float32)
    picked_grad = send_back(d_partial.reshape(owners, local_experts * slot_cap, width))
    grad_tokens = jnp.sum(picked_grad.astype(jnp.float32), axis=1).astype(jnp.bfloat16)
    grad_probs = lax.psum(prob_part, "col")
    return (mixed, grad_tokens, grad_probs, grad_gate, grad_up, grad_down)


def solution(mesh):
    return jax.shard_map(
        body,
        mesh=mesh,
        in_specs=(
            P("dp", None),
            P("dp", None),
            P("dp", None),
            P("dp", None, "col"),
            P("dp", None, "col"),
            P("dp", "col", None),
            P("dp", "col"),
        ),
        out_specs=(
            P("dp", "col"),
            P("dp", "col"),
            P("dp", None),
            P("dp", None, "col"),
            P("dp", None, "col"),
            P("dp", "col", None),
        ),
        check_vma=False,
    )
```

profile of v0, /device:TPU:82, one launch (start us, length us, event | category | flops | bytes accessed | tf_op | source)
XLA Modules:
  0.0 683.6 jit_solution(13827045977689101927)
XLA Ops:
  10.4 1.1 broadcast_add_fusion
  12.0 10.6 %scatter_custom_fusion = bf16[1536,2048]{1,0:T(8,128)(2,1)} fusion(s32[1024]{0:T(1024)S(1)} %bitcast.136, bf16[]{:T(256)} %constant.6.clone.1, bf16[128,2048]{1,0:T(8,128)(2,1)} %param.7), kind=kCustom, calls=%fused_computation.15 | custom fusion | bytes 6815746 | tf_op jit(solution)/shard_map/scatter | solution.py:24
  22.6 10.9 %all-to-all-start = ((bf16[64,24,2048]{2,1,0:T(8,128)(2,1)}), bf16[64,24,2048]{2,1,0:T(8,128)(2,1)}, u32[]{:S(2)}, u32[]{:S(2)}) async-start(bf16[64,24,2048]{2,1,0:T(8,128)(2,1)} %bitcast.126), calls=%async_computation | async-start | bytes 12582912 | tf_op jit(solution)/shard_map/all_to_all | solution.py:28
  33.7 88.8 %all_gather.3 = bf16[128,2048]{1,0:T(8,128)(2,1)S(1)} all-gather(bf16[128,1024]{1,0:T(8,128)(2,1)S(1)} %copy-done.11), channel_id=1, replica_groups=mesh['dp'=64,'col'=2] {'col'}, dimensions={1}, use_global_device_ids=true | all-gather | bytes 786432 | tf_op jit(solution)/shard_map/all_gather | solution.py:54
  123.5 11.0 %scatter_custom_fusion.1 = bf16[1536,2048]{1,0:T(8,128)(2,1)} fusion(s32[1024]{0:T(1024)S(1)} %bitcast.137, f32[128,2048]{1,0:T(8,128)} %convert_element_type.63, f32[1024]{0:T(1024)S(1)} %mul.86, bf16[]{:T(256)} %constant.6.clone.1), kind=kCustom, calls=%fused_computation.14 | custom fusion | flops 4194304 | bytes 7344130 | tf_op jit(solution)/shard_map/scatter | solution.py:24
  134.6 9.1 %all-to-all-start.2 = ((bf16[64,24,2048]{2,1,0:T(8,128)(2,1)}), bf16[64,24,2048]{2,1,0:T(8,128)(2,1)}, u32[]{:S(2)}, u32[]{:S(2)}) async-start(bf16[64,24,2048]{2,1,0:T(8,128)(2,1)} %bitcast.125), calls=%async_computation.3 | async-start | bytes 12582912 | tf_op jit(solution)/shard_map/all_to_all | solution.py:28
  143.9 6.4 copy.33
  150.3 4.8 fusion.10
  155.1 4.8 fusion.14
  160.0 68.8 %all-to-all-done.2 = bf16[64,24,2048]{2,1,0:T(8,128)(2,1)} async-done(((bf16[64,24,2048]{2,1,0:T(8,128)(2,1)}), bf16[64,24,2048]{2,1,0:T(8,128)(2,1)}, u32[]{:S(2)}, u32[]{:S(2)}) %all-to-all-start.2) | async-done | bytes 6291488 | tf_op jit(solution)/shard_map/all_to_all | solution.py:28
  228.8 6.4 copy.36
  235.2 6.0 fusion.25
  241.2 4.9 fusion.12
  246.1 7.7 %convolution_add_fusion = f32[2,64,12,2048]{3,1,2,0:T(8,128)} fusion(f32[2,64,12,2048]{3,1,2,0:T(8,128)S(1)} %fusion.12, bf16[64,2,12,384]{3,0,2,1:T(8,128)(2,1)} %get-tuple-element.14, bf16[2,2048,384]{2,1,0:T(8,128)(2,1)S(1)} %copy-done.7), kind=kOutput, calls=%fused_computation.9 | convolution fusion | flops 2419064832 | bytes 29491200 | tf_op jit(solution)/shard_map/slch,ldh->slcd/dot_general | solution.py:76
  253.9 16.4 %copy.37 = f32[64,24,2048]{2,1,0:T(8,128)} copy(f32[64,24,2048]{2,0,1:T(8,128)} %bitcast.124) | data formatting | bytes 25165824 | tf_op jit(solution)/shard_map/reshape | solution.py:77
  270.3 7.9 %fusion.18 = f32[2,64,12,2048]{3,1,2,0:T(8,128)} fusion(bf16[64,2,12,384]{3,0,2,1:T(8,128)(2,1)} %get-tuple-element.16, bf16[2,384,2048]{2,1,0:T(8,128)(2,1)S(1)} %copy-done), kind=kOutput, calls=%fused_computation.28 | convolution fusion | flops 2415919104 | bytes 16908288 | tf_op jit(solution)/shard_map/slch,lhd->slcd/dot_general | solution.py:48
  278.3 17.2 %copy.34 = f32[64,24,2048]{2,1,0:T(8,128)} copy(f32[64,24,2048]{2,0,1:T(8,128)} %bitcast.123) | data formatting | bytes 25165824 | tf_op jit(solution)/shard_map/reshape | solution.py:49
  295.5 121.4 %reduce-scatter.5.cloned.1.call-done = f32[64,24,1024]{2,1,0:T(8,128)} async-done(((f32[64,24,2048]{2,1,0:T(8,128)}), f32[64,24,1024]{2,1,0:T(8,128)}) %reduce-scatter.5.cloned.1.call-update) | async-done | bytes 6291472 | tf_op jit(solution)/shard_map/reduce_scatter | solution.py:33
  416.9 4.9 convert_element_type.67
  421.8 10.4 %all-to-all-start.3 = ((bf16[64,24,1024]{2,1,0:T(8,128)(2,1)}), bf16[64,24,1024]{2,1,0:T(8,128)(2,1)S(1)}, u32[]{:S(2)}, u32[]{:S(2)}) async-start(bf16[64,24,1024]{2,1,0:T(8,128)(2,1)} %convert_element_type.67), calls=%async_computation.5 | async-start | bytes 6291456 | tf_op jit(solution)/shard_map/all_to_all | solution.py:36
  433.1 168.6 %reduce-scatter.3.cloned.1.call-done = f32[64,24,1024]{2,1,0:T(8,128)} async-done(((f32[64,24,2048]{2,1,0:T(8,128)}), f32[64,24,1024]{2,1,0:T(8,128)}) %reduce-scatter.3.cloned.1.call-update) | async-done | bytes 6291472 | tf_op jit(solution)/shard_map/reduce_scatter | solution.py:33
  601.7 4.9 convert_element_type.59
  606.6 10.5 %all-to-all-start.1 = ((bf16[64,24,1024]{2,1,0:T(8,128)(2,1)}), bf16[64,24,1024]{2,1,0:T(8,128)(2,1)}, u32[]{:S(2)}, u32[]{:S(2)}) async-start(bf16[64,24,1024]{2,1,0:T(8,128)(2,1)} %convert_element_type.59), calls=%async_computation.2 | async-start | bytes 6291456 | tf_op jit(solution)/shard_map/all_to_all | solution.py:36
  617.2 7.6 %bitcast_convert_fusion = bf16[2,384,2048]{2,1,0:T(8,128)(2,1)} fusion(bf16[64,2,12,384]{3,0,2,1:T(8,128)(2,1)} %get-tuple-element.16, bf16[64,2,12,2048]{3,0,2,1:T(8,128)(2,1)} %bitcast.134), kind=kOutput, calls=%fused_computation.6 | convolution fusion | flops 2417491968 | bytes 10616832 | tf_op jit(solution)/shard_map/slch,slcd->lhd/dot_general | solution.py:60
  624.8 8.1 %bitcast_convert_fusion.1 = bf16[2,2048,384]{2,1,0:T(8,128)(2,1)} fusion(bf16[64,2,12,2048]{3,0,2,1:T(8,128)(2,1)} %bitcast.129, bf16[64,2,12,384]{3,0,2,1:T(8,128)(2,1)S(1)} %copy-done.10), kind=kOutput, calls=%fused_computation.7 | convolution fusion | flops 2417491968 | bytes 10616832 | tf_op jit(solution)/shard_map/slcd,slch->ldh/dot_general | solution.py:71
  632.9 4.9 bitcast_convert_fusion.2
  637.8 5.4 gather_fusion.1
  643.2 3.7 bitcast_reduce_fusion
  646.9 9.0 %all-to-all-done.1 = bf16[64,24,1024]{2,1,0:T(8,128)(2,1)} async-done(((bf16[64,24,1024]{2,1,0:T(8,128)(2,1)}), bf16[64,24,1024]{2,1,0:T(8,128)(2,1)}, u32[]{:S(2)}, u32[]{:S(2)}) %all-to-all-start.1) | async-done | bytes 3145760 | tf_op jit(solution)/shard_map/all_to_all | solution.py:36
  656.0 8.5 %gather_fusion = bf16[1024,1024]{1,0:T(8,128)(2,1)} fusion(bf16[1536,1024]{1,0:T(8,128)(2,1)} %bitcast.18, s32[1024]{0:T(1024)S(1)} %broadcast_clamp_fusion), kind=kCustom, calls=%fused_computation | custom fusion | bytes 4198400 | tf_op jit(solution)/shard_map/gather | solution.py:37
  664.5 4.1 fusion.2
  668.5 7.3 %psum.7 = f32[128,8]{1,0:T(8,128)S(1)} all-reduce(f32[128,8]{1,0:T(8,128)S(1)} %get-tuple-element.12), channel_id=1, replica_groups=mesh['dp'=64,'col'=2] {'col'}, use_global_device_ids=true, to_apply=%region_10.11 | all-reduce | flops 1024 | bytes 8192 | tf_op jit(solution)/shard_map/psum | solution.py:79
  (61 shorter events, 6.9 us)
Async XLA Ops:
  7.2 228.0 %copy-start = (bf16[2,384,2048]{2,1,0:T(8,128)(2,1)S(1)}, bf16[2,384,2048]{2,1,0:T(8,128)(2,1)}, u32[]{:S(2)}) copy-start(bf16[2,384,2048]{2,1,0:T(8,128)(2,1)} %param.12) | copy-start | bytes 9437188
  9.6 0.8 copy-start.8
  22.6 10.9 %copy-start.12 = (f32[128,8]{0,1:T(8,128)S(1)}, f32[128,8]{0,1:T(8,128)}, u32[]{:S(2)}) copy-start(f32[128,8]{0,1:T(8,128)} %param.9) | copy-start | bytes 12292
  22.6 11.1 %copy-start.11 = (bf16[128,1024]{1,0:T(8,128)(2,1)S(1)}, bf16[128,1024]{1,0:T(8,128)(2,1)}, u32[]{:S(2)}) copy-start(bf16[128,1024]{1,0:T(8,128)(2,1)} %param.13) | copy-start | bytes 786436
  22.6 112.0 %all-to-all-start = ((bf16[64,24,2048]{2,1,0:T(8,128)(2,1)}), bf16[64,24,2048]{2,1,0:T(8,128)(2,1)}, u32[]{:S(2)}, u32[]{:S(2)}) async-start(bf16[64,24,2048]{2,1,0:T(8,128)(2,1)} %bitcast.126), calls=%async_computation | async-start | bytes 12582912 | tf_op jit(solution)/shard_map/all_to_all | solution.py:28
  134.6 94.2 %all-to-all-start.2 = ((bf16[64,24,2048]{2,1,0:T(8,128)(2,1)}), bf16[64,24,2048]{2,1,0:T(8,128)(2,1)}, u32[]{:S(2)}, u32[]{:S(2)}) async-start(bf16[64,24,2048]{2,1,0:T(8,128)(2,1)} %bitcast.125), calls=%async_computation.3 | async-start | bytes 12582912 | tf_op jit(solution)/shard_map/all_to_all | solution.py:28
  143.6 273.3 %reduce-scatter.5.cloned.1.call-start = ((), (), s32[]{:S(2)}) async-start(), calls=%async_computation.7 | async-start | bytes 18874368 | tf_op jit(solution)/shard_map/reduce_scatter | solution.py:33
  143.9 6.4 copy-start.6
  150.3 4.8 copy-start.2
  150.3 4.8 copy-start.4
  228.8 6.4 copy-start.13
  228.8 6.4 copy-start.14
  235.2 6.1 copy-start.3
  235.2 6.0 copy-start.5
  241.2 4.9 copy-start.7
  270.3 331.4 %reduce-scatter.3.cloned.1.call-start = ((), (), s32[]{:S(2)}) async-start(), calls=%async_computation.6 | async-start | bytes 18874368 | tf_op jit(solution)/shard_map/reduce_scatter | solution.py:33
  421.8 184.8 %all-to-all-start.3 = ((bf16[64,24,1024]{2,1,0:T(8,128)(2,1)}), bf16[64,24,1024]{2,1,0:T(8,128)(2,1)S(1)}, u32[]{:S(2)}, u32[]{:S(2)}) async-start(bf16[64,24,1024]{2,1,0:T(8,128)(2,1)} %convert_element_type.67), calls=%async_computation.5 | async-start | bytes 6291456 | tf_op jit(solution)/shard_map/all_to_all | solution.py:36
  606.6 49.3 %all-to-all-start.1 = ((bf16[64,24,1024]{2,1,0:T(8,128)(2,1)}), bf16[64,24,1024]{2,1,0:T(8,128)(2,1)}, u32[]{:S(2)}, u32[]{:S(2)}) async-start(bf16[64,24,1024]{2,1,0:T(8,128)(2,1)} %convert_element_type.59), calls=%async_computation.2 | async-start | bytes 6291456 | tf_op jit(solution)/shard_map/all_to_all | solution.py:36
  617.2 7.6 %copy-start.10 = (bf16[64,2,12,384]{3,0,2,1:T(8,128)(2,1)S(1)}, bf16[64,2,12,384]{3,0,2,1:T(8,128)(2,1)}, u32[]{:S(2)}) copy-start(bf16[64,2,12,384]{3,0,2,1:T(8,128)(2,1)} %get-tuple-element.14) | copy-start | bytes 3538948
  617.2 15.7 %slice-start = ((s8[6291456]{0:T(1024)(128)(4,1)}), s8[4194304]{0:T(1024)(128)(4,1)S(1)}, s32[]{:S(2)}) async-start(s8[6291456]{0:T(1024)(128)(4,1)} %bitcast.130), calls=%async_computation.8 | async-start | bytes 8388608
  624.8 8.1 %slice-start.1 = ((s8[6291456]{0:T(1024)(128)(4,1)}), s8[2097152]{0:T(1024)(128)(4,1)S(1)}, s32[]{:S(2)}) async-start(s8[6291456]{0:T(1024)(128)(4,1)} %bitcast.130), calls=%async_computation.9 | async-start | bytes 4194304
  624.8 8.1 %copy-start.9 = (bf16[64,2,12,384]{3,0,2,1:T(8,128)(2,1)S(1)}, bf16[64,2,12,384]{3,0,2,1:T(8,128)(2,1)}, u32[]{:S(2)}) copy-start(bf16[64,2,12,384]{3,0,2,1:T(8,128)(2,1)} %get-tuple-element.15) | copy-start | bytes 3538948
  656.0 20.6 %copy-start.1 = (bf16[2,384,2048]{2,1,0:T(8,128)(2,1)S(1)}, bf16[2,384,2048]{2,1,0:T(8,128)(2,1)}, u32[]{:S(2)}) copy-start(bf16[2,384,2048]{2,1,0:T(8,128)(2,1)} %param.12) | copy-start | bytes 9437188
Sparse Core Ops, SparseCore 0:
  270.4 146.4 reduce-scatter.4
  419.3 182.3 reduce-scatter.2
where the time goes:
time: 694 us; the launch traced here: 684 us
  waiting for transfers between devices  368 us (53%)
  blocking collectives  96.1 us (14%)
  local copies, waits for them, and re-layouts  74.1 us (11%)
  matrix products  56.8 us (8%)
  starting transfers between devices  41.1 us (6%)
  other arithmetic  33.1 us (5%)
  between operations  14.5 us (2%)
    reduce_scatter x2, waiting for transfers between devices, send_back(): lax.psum_scatter(partial_value, 'col', scatter_dimension=2, tiled=True)  290 us
    all_gather x1, blocking collectives, body(): full_cot = lax.all_gather(cotangent, 'col', axis=1, tiled=True)  88.8 us
    all_to_all x2, waiting for transfers between devices, send_whole(): lax.all_to_all(scatter_rows(row_pairs), 'dp', split_axis=0, concat_axis=0...  68.8 us
    all_to_all x2, starting transfers between devices, send_back(): lax.all_to_all(summed, 'dp', split_axis=0, concat_axis=0, tiled=True)  20.9 us
    all_to_all x2, starting transfers between devices, send_whole(): lax.all_to_all(scatter_rows(row_pairs), 'dp', split_axis=0, concat_axis=0...  19.9 us
    reshape x1, local copies, waits for them, and re-layouts, body(): out_partial.reshape(owners, local_experts * slot_cap, width)  17.2 us
    reshape x1, local copies, waits for them, and re-layouts, body(): d_partial.reshape(owners, local_experts * slot_cap, width)  16.4 us
  transfers between devices with their start and end apart: 6, of which 4 were waited for; matrix products, arithmetic and copies ran while one was open for 14% of the time, Pallas kernels for 0%

commit v1 on v0

v1 whole, which is shorter than its diff:
```python
import jax
import jax.numpy as jnp
from jax import lax
from jax.sharding import PartitionSpec as P


def body(tokens, routes, probs, w_gate, w_up, w_down, cotangent):
    tok_count, width = tokens.shape
    top_count = routes.shape[1]
    owners = lax.axis_size("dp")
    cols = lax.axis_size("col")
    local_experts = w_gate.shape[0]
    experts = local_experts * owners
    slot_cap = 3 * tok_count * top_count // (2 * experts)
    half_width = width // cols
    pair_count = tok_count * top_count
    rows_per_owner = local_experts * slot_cap
    slots = experts * slot_cap

    flat_routes = routes.reshape(-1)
    expert_ids = jnp.arange(experts, dtype=jnp.int32)
    onehot = (flat_routes[:, None] == expert_ids[None, :]).astype(jnp.int32)
    before = jnp.cumsum(onehot, axis=0) - onehot
    slot_index = jnp.sum(before * onehot, axis=1)
    flat_index = flat_routes * slot_cap + slot_index

    pair_of_slot = jnp.full((slots,), pair_count, jnp.int32).at[flat_index].set(
        jnp.arange(pair_count, dtype=jnp.int32)
    )
    valid = pair_of_slot < pair_count
    safe_pair = jnp.where(valid, pair_of_slot, 0)
    token_of_slot = safe_pair // top_count

    both = ("dp", "col")

    send_tok = jnp.where(valid[:, None], tokens[token_of_slot], jnp.zeros((), tokens.dtype))
    arrived_rows = lax.all_to_all(
        send_tok.reshape(owners, rows_per_owner, width), "dp", 0, 0, tiled=True
    )
    row_block = arrived_rows.reshape(owners, local_experts, slot_cap, width)

    prob_of_slot = jnp.where(valid, probs.reshape(-1)[safe_pair], 0.0)
    send_cot = (prob_of_slot[:, None] * cotangent[token_of_slot].astype(jnp.float32)).astype(
        jnp.bfloat16
    )
    send_cot = jnp.broadcast_to(
        send_cot.reshape(owners, 1, rows_per_owner, half_width),
        (owners, cols, rows_per_owner, half_width),
    ).reshape(owners * cols, rows_per_owner, half_width)
    arrived_cot = lax.all_to_all(send_cot, both, 0, 0, tiled=True)
    d_out = (
        arrived_cot.reshape(owners, cols, rows_per_owner, half_width)
        .transpose(0, 2, 1, 3)
        .reshape(owners, local_experts, slot_cap, width)
    )

    def send_back(partial_value):
        part = partial_value.astype(jnp.bfloat16).reshape(owners, rows_per_owner, cols, half_width)
        part = part.transpose(0, 2, 1, 3).reshape(owners * cols, rows_per_owner, half_width)
        got = lax.all_to_all(part, both, 0, 0, tiled=True)
        got = got.reshape(owners, cols, rows_per_owner, half_width).astype(jnp.float32)
        summed = jnp.sum(got, axis=1).reshape(slots, half_width)
        return summed[flat_index].reshape(tok_count, top_count, half_width)

    gate_acts = jnp.einsum("slcd,ldh->slch", row_block, w_gate, preferred_element_type=jnp.float32)
    up_acts = jnp.einsum("slcd,ldh->slch", row_block, w_up, preferred_element_type=jnp.float32)
    sigmoid_g = jax.nn.sigmoid(gate_acts)
    silu_g = gate_acts * sigmoid_g
    hidden = (silu_g * up_acts).astype(jnp.bfloat16)
    out_partial = jnp.einsum("slch,lhd->slcd", hidden, w_down, preferred_element_type=jnp.float32)
    picked_wide = send_back(out_partial)
    mixed = jnp.sum(probs[:, :, None] * picked_wide, axis=1).astype(jnp.bfloat16)
    cot_wide = cotangent.astype(jnp.float32)
    prob_part = jnp.sum(cot_wide[:, None, :] * picked_wide, axis=2)

    grad_down = jnp.einsum(
        "slch,slcd->lhd", hidden, d_out, preferred_element_type=jnp.float32
    ).astype(jnp.bfloat16)
    d_hidden = jnp.einsum("slcd,lhd->slch", d_out, w_down, preferred_element_type=jnp.float32)
    d_gate = (d_hidden * up_acts * sigmoid_g * (1.0 + gate_acts * (1.0 - sigmoid_g))).astype(
        jnp.bfloat16
    )
    d_up = (d_hidden * silu_g).astype(jnp.bfloat16)
    grad_gate = jnp.einsum(
        "slcd,slch->ldh", row_block, d_gate, preferred_element_type=jnp.float32
    ).astype(jnp.bfloat16)
    grad_up = jnp.einsum(
        "slcd,slch->ldh", row_block, d_up, preferred_element_type=jnp.float32
    ).astype(jnp.bfloat16)
    d_partial = jnp.einsum(
        "slch,ldh->slcd", d_gate, w_gate, preferred_element_type=jnp.float32
    ) + jnp.einsum("slch,ldh->slcd", d_up, w_up, preferred_element_type=jnp.float32)
    picked_grad = send_back(d_partial)
    grad_tokens = jnp.sum(picked_grad, axis=1).astype(jnp.bfloat16)
    grad_probs = lax.psum(prob_part, "col")
    return (mixed, grad_tokens, grad_probs, grad_gate, grad_up, grad_down)


def solution(mesh):
    return jax.shard_map(
        body,
        mesh=mesh,
        in_specs=(
            P("dp", None),
            P("dp", None),
            P("dp", None),
            P("dp", None, "col"),
            P("dp", None, "col"),
            P("dp", "col", None),
            P("dp", "col"),
        ),
        out_specs=(
            P("dp", "col"),
            P("dp", "col"),
            P("dp", None),
            P("dp", None, "col"),
            P("dp", None, "col"),
            P("dp", "col", None),
        ),
        check_vma=False,
    )
```

time: 694 us -> 495 us (0.71)
  waiting for transfers between devices: 368 us -> 171 us
  local copies, waits for them, and re-layouts: 74.1 us -> 135 us
  blocking collectives: 96.1 us -> 41.6 us
  between operations: 14.5 us -> 1.41 us
    reduce_scatter x2 -> x0, waiting for transfers between devices: 290 us -> none  [send_back(): lax.psum_scatter(partial_value, 'col', scatter_dimension=2, tiled=True)]
    all_to_all x4, waiting for transfers between devices: 77.8 us -> 171 us  [the longest x1 69 us: body(): lax.all_to_all(send_tok.reshape(owners, rows_per_owner, width), 'dp', 0,...]
    all_gather x1 -> x0, blocking collectives: 88.8 us -> none  [body(): full_cot = lax.all_gather(cotangent, 'col', axis=1, tiled=True)]
    psum x1, blocking collectives: 7.34 us -> 41.6 us  [body(): grad_probs = lax.psum(prob_part, 'col')]
    gather x2 -> x5, local copies, waits for them, and re-layouts: 13.9 us -> 44.2 us  [the longest x2 18.7 us: send_back(): return summed[flat_index].reshape(tok_count, top_count, half_width)]
    transpose x0 -> x2, local copies, waits for them, and re-layouts: none -> 24.3 us  [send_back(): part.transpose(0, 2, 1, 3)]
    reduce_sum x1 -> x3, other arithmetic: 3.73 us -> 19.9 us  [the longest x2 15.9 us: send_back(): summed = jnp.sum(got, axis=1).reshape(slots, half_width)]
    reshape x2 -> x5, local copies, waits for them, and re-layouts: 33.6 us -> 46.5 us  [the longest x2 22.3 us: send_back(): partial_value.astype(jnp.bfloat16)]
  transfers between devices with their start and end apart: 6 -> 4, of which waited for: 4 -> 3; matrix products, arithmetic and copies ran while one was open for 14% -> 23% of each run, Pallas kernels for 0% -> 0%
where the time goes in v1:
time: 495 us; the launch traced here: 488 us
  waiting for transfers between devices  171 us (35%)
  local copies, waits for them, and re-layouts  135 us (27%)
  matrix products  60.8 us (12%)
  blocking collectives  41.6 us (8%)
  starting transfers between devices  40 us (8%)
  other arithmetic  37 us (7%)
    all_to_all x1, waiting for transfers between devices, body(): lax.all_to_all(send_tok.reshape(owners, rows_per_owner, width), 'dp', 0,...  69 us
    all_to_all x1, waiting for transfers between devices, body(): arrived_cot = lax.all_to_all(send_cot, both, 0, 0, tiled=True)  62.7 us
    psum x1, blocking collectives, body(): grad_probs = lax.psum(prob_part, 'col')  41.6 us
    all_to_all x2, waiting for transfers between devices, send_back(): got = lax.all_to_all(part, both, 0, 0, tiled=True)  39.6 us
    transpose x2, local copies, waits for them, and re-layouts, send_back(): part.transpose(0, 2, 1, 3)  24.3 us
    reshape x2, local copies, waits for them, and re-layouts, send_back(): partial_value.astype(jnp.bfloat16)  22.3 us
    all_to_all x2, starting transfers between devices, send_back(): got = lax.all_to_all(part, both, 0, 0, tiled=True)  20.1 us
    gather x2, local copies, waits for them, and re-layouts, send_back(): return summed[flat_index].reshape(tok_count, top_count, half_width)  18.7 us
  transfers between devices with their start and end apart: 4, of which 3 were waited for; matrix products, arithmetic and copies ran while one was open for 23% of the time, Pallas kernels for 0%

profile of v1, /device:TPU:82, one launch (start us, length us, event | category | flops | bytes accessed | tf_op | source)
XLA Modules:
  0.0 487.6 jit_solution(17943085556747740013)
XLA Ops:
  10.0 13.8 %gather_fusion = bf16[1536,2048]{1,0:T(8,128)(2,1)} fusion(bf16[128,2048]{1,0:T(8,128)(2,1)} %param.7, s32[2048]{0:T(1024)S(1)} %pad_clamp_fusion.1), kind=kCustom, calls=%fused_computation | custom fusion | bytes 12589056 | tf_op jit(solution)/shard_map/gather | solution.py:36
  23.8 5.9 %broadcast_select_fusion = bf16[64,24,2048]{2,1,0:T(8,128)(2,1)} fusion(bf16[64,24,2048]{2,1,0:T(8,128)(2,1)} %bitcast.147, pred[64,24]{1,0:T(8,128)(4,1)S(1)} %broadcast_in_dim.42), kind=kLoop, calls=%fused_computation.17 | loop fusion | flops 3145728 | bytes 12584448 | tf_op jit(solution)/shard_map/jit(_where)/select_n | solution.py:36
  29.7 10.9 %all-to-all-start = ((bf16[64,24,2048]{2,1,0:T(8,128)(2,1)}), bf16[64,24,2048]{2,1,0:T(8,128)(2,1)}, u32[]{:S(2)}, u32[]{:S(2)}) async-start(bf16[64,24,2048]{2,1,0:T(8,128)(2,1)} %broadcast_select_fusion), calls=%async_computation | async-start | bytes 12582912 | tf_op jit(solution)/shard_map/all_to_all | solution.py:37
  40.8 5.9 %gather_fusion.2 = f32[1536]{0:T(1024)S(1)} fusion(f32[1024]{0:T(1024)S(1)} %reshape.147, s32[2048]{0:T(1024)S(1)} %pad_clamp_fusion), kind=kCustom, calls=%fused_computation.2 | custom fusion | bytes 18432 | tf_op jit(solution)/shard_map/gather | solution.py:42
  46.8 5.8 %gather_fusion.3 = bf16[1536,1024]{1,0:T(8,128)(2,1)} fusion(bf16[128,1024]{1,0:T(8,128)(2,1)S(1)} %copy-done.2, s32[2048]{0:T(1024)S(1)} %pad_clamp_fusion.1), kind=kCustom, calls=%fused_computation.3 | custom fusion | bytes 6297600 | tf_op jit(solution)/shard_map/gather | solution.py:43
  56.7 69.0 %all-to-all-done = bf16[64,24,2048]{2,1,0:T(8,128)(2,1)} async-done(((bf16[64,24,2048]{2,1,0:T(8,128)(2,1)}), bf16[64,24,2048]{2,1,0:T(8,128)(2,1)}, u32[]{:S(2)}, u32[]{:S(2)}) %all-to-all-start) | async-done | bytes 6291488 | tf_op jit(solution)/shard_map/all_to_all | solution.py:37
  125.7 5.4 %broadcast_in_dim.49 = bf16[64,2,24,1024]{3,2,1,0:T(8,128)(2,1)} broadcast(bf16[64,24,1024]{2,1,0:T(8,128)(2,1)} %fusion.1), dimensions={0,2,3} | broadcast | bytes 9437184 | tf_op jit(solution)/shard_map/broadcast_in_dim | solution.py:46
  131.1 9.0 %all-to-all-start.2 = ((bf16[128,24,1024]{2,1,0:T(8,128)(2,1)}), bf16[128,24,1024]{2,1,0:T(8,128)(2,1)}, u32[]{:S(2)}, u32[]{:S(2)}) async-start(bf16[128,24,1024]{2,1,0:T(8,128)(2,1)} %bitcast.143), calls=%async_computation.2 | async-start | bytes 12582912 | tf_op jit(solution)/shard_map/all_to_all | solution.py:50
  140.2 6.4 %copy.32 = bf16[64,24,2048]{2,0,1:T(8,128)(2,1)S(1)} copy(bf16[64,24,2048]{2,1,0:T(8,128)(2,1)} %all-to-all-done) | data formatting | bytes 12582912 | tf_op jit(solution)/shard_map/all_to_all | solution.py:37
  146.6 4.8 fusion.5
  156.2 62.7 %all-to-all-done.2 = bf16[128,24,1024]{2,1,0:T(8,128)(2,1)} async-done(((bf16[128,24,1024]{2,1,0:T(8,128)(2,1)}), bf16[128,24,1024]{2,1,0:T(8,128)(2,1)}, u32[]{:S(2)}, u32[]{:S(2)}) %all-to-all-start.2) | async-done | bytes 6291488 | tf_op jit(solution)/shard_map/all_to_all | solution.py:50
  219.0 12.6 %copy.51 = bf16[64,2,24,1024]{3,1,0,2:T(2,128)(2,1)} copy(bf16[64,2,24,1024]{3,2,1,0:T(8,128)(2,1)} %bitcast.23) | data formatting | bytes 12582912 | tf_op jit(solution)/shard_map/reshape | solution.py:52
  231.6 11.5 %reshape.150 = bf16[64,2,12,2048]{3,0,2,1:T(8,128)(2,1)} reshape(bf16[64,24,2,1024]{3,2,0,1:T(2,128)(2,1)} %bitcast.144) | data formatting | bytes 12582912 | tf_op jit(solution)/shard_map/reshape | solution.py:54
  243.1 9.7 %fusion.17 = (bf16[64,2,12,384]{3,0,2,1:T(8,128)(2,1)}, bf16[64,2,12,384]{3,0,2,1:T(8,128)(2,1)}, bf16[64,2,12,384]{3,0,2,1:T(8,128)(2,1)S(1)}) fusion(f32[2,64,12,384]{3,1,2,0:T(8,128)} %fusion.9, f32[2,64,12,384]{3,1,2,0:T(8,128)} %fusion.5, bf16[64,2,12,2048]{3,0,2,1:T(8,128)(2,1)} %reshape.150, bf16[2,384,2048]{2,1,0:T(8,128)(2,1)S(1)} %copy-done), kind=kOutput, calls=%fused_computation.38 | convolution fusion | flops 2424766464 | bytes 17694720 | tf_op jit(solution)/shard_map/slcd,lhd->slch/dot_general | solution.py:79
  253.8 5.3 %convert_bitcast_fusion = bf16[64,2,12,2048]{3,0,2,1:T(8,128)(2,1)} fusion(bf16[64,2,12,384]{3,0,2,1:T(8,128)(2,1)S(1)} %get-tuple-element.18, bf16[2,384,2048]{2,1,0:T(8,128)(2,1)S(1)} %copy-done), kind=kOutput, calls=%fused_computation.16 | convolution fusion | flops 2419064832 | bytes 10616832 | tf_op jit(solution)/shard_map/slch,lhd->slcd/dot_general | solution.py:70
  259.2 11.2 %reshape.143 = bf16[64,24,2,1024]{3,2,0,1:T(2,128)(2,1)} reshape(bf16[64,2,12,2048]{3,0,2,1:T(8,128)(2,1)} %convert_bitcast_fusion) | data formatting | bytes 12582912 | tf_op jit(solution)/shard_map/reshape | solution.py:58
  270.3 12.2 %copy.33 = bf16[64,2,24,1024]{3,2,1,0:T(8,128)(2,1)} copy(bf16[64,2,24,1024]{3,1,0,2:T(2,128)(2,1)} %bitcast.145) | data formatting | bytes 12582912 | tf_op jit(solution)/shard_map/transpose | solution.py:59
  282.5 10.0 %all-to-all-start.1 = ((bf16[128,24,1024]{2,1,0:T(8,128)(2,1)}), bf16[128,24,1024]{2,1,0:T(8,128)(2,1)}, u32[]{:S(2)}, u32[]{:S(2)}) async-start(bf16[128,24,1024]{2,1,0:T(8,128)(2,1)} %bitcast.142), calls=%async_computation.1 | async-start | bytes 12582912 | tf_op jit(solution)/shard_map/all_to_all | solution.py:60
  292.6 7.7 %fusion.7 = f32[2,64,12,2048]{3,1,2,0:T(8,128)} fusion(bf16[64,2,12,384]{3,0,2,1:T(8,128)(2,1)} %get-tuple-element.17, bf16[2,2048,384]{2,1,0:T(8,128)(2,1)S(1)} %copy-done.5), kind=kOutput, calls=%fused_computation.26 | convolution fusion | flops 2415919104 | bytes 16908288 | tf_op jit(solution)/shard_map/slch,ldh->slcd/dot_general | solution.py:90
  300.3 8.1 %fusion = bf16[64,2,12,2048]{3,0,2,1:T(8,128)(2,1)} fusion(f32[2,64,12,2048]{3,1,2,0:T(8,128)} %fusion.7, bf16[64,2,12,384]{3,0,2,1:T(8,128)(2,1)S(1)} %copy-done.10, bf16[2,2048,384]{2,1,0:T(8,128)(2,1)S(1)} %copy-done.7), kind=kOutput, calls=%fused_computation.9 | convolution fusion | flops 2422210560 | bytes 23199744 | tf_op jit(solution)/shard_map/slch,ldh->slcd/dot_general | solution.py:92
  308.4 11.1 %reshape.151 = bf16[64,24,2,1024]{3,2,0,1:T(2,128)(2,1)} reshape(bf16[64,2,12,2048]{3,0,2,1:T(8,128)(2,1)} %fusion) | data formatting | bytes 12582912 | tf_op jit(solution)/shard_map/reshape | solution.py:58
  319.6 12.1 %copy.38 = bf16[64,2,24,1024]{3,2,1,0:T(8,128)(2,1)} copy(bf16[64,2,24,1024]{3,1,0,2:T(2,128)(2,1)} %bitcast.146) | data formatting | bytes 12582912 | tf_op jit(solution)/shard_map/transpose | solution.py:59
  331.7 39.6 %all-to-all-done.1 = bf16[128,24,1024]{2,1,0:T(8,128)(2,1)} async-done(((bf16[128,24,1024]{2,1,0:T(8,128)(2,1)}), bf16[128,24,1024]{2,1,0:T(8,128)(2,1)}, u32[]{:S(2)}, u32[]{:S(2)}) %all-to-all-start.1) | async-done | bytes 6291488 | tf_op jit(solution)/shard_map/all_to_all | solution.py:60
  371.3 10.0 %all-to-all-start.3 = ((bf16[128,24,1024]{2,1,0:T(8,128)(2,1)}), bf16[128,24,1024]{2,1,0:T(8,128)(2,1)}, u32[]{:S(2)}, u32[]{:S(2)}) async-start(bf16[128,24,1024]{2,1,0:T(8,128)(2,1)} %bitcast.141), calls=%async_computation.3 | async-start | bytes 12582912 | tf_op jit(solution)/shard_map/all_to_all | solution.py:60
  381.5 7.3 %bitcast_convert_fusion = bf16[2,384,2048]{2,1,0:T(8,128)(2,1)} fusion(bf16[64,2,12,384]{3,0,2,1:T(8,128)(2,1)S(1)} %copy-done.14, bf16[64,2,12,2048]{3,0,2,1:T(8,128)(2,1)} %reshape.150), kind=kOutput, calls=%fused_computation.12 | convolution fusion | flops 2417491968 | bytes 10616832 | tf_op jit(solution)/shard_map/slch,slcd->lhd/dot_general | solution.py:76
  388.7 8.1 %bitcast_convert_fusion.1 = bf16[2,2048,384]{2,1,0:T(8,128)(2,1)} fusion(bf16[64,2,12,2048]{3,0,2,1:T(8,128)(2,1)} %bitcast.151, bf16[64,2,12,384]{3,0,2,1:T(8,128)(2,1)S(1)} %copy-done.11), kind=kOutput, calls=%fused_computation.13 | convolution fusion | flops 2417491968 | bytes 10616832 | tf_op jit(solution)/shard_map/slcd,slch->ldh/dot_general | solution.py:87
  396.8 4.9 %bitcast_convert_fusion.2 = bf16[2,2048,384]{2,1,0:T(8,128)(2,1)} fusion(bf16[64,2,12,2048]{3,0,2,1:T(8,128)(2,1)S(1)} %bitcast.154, bf16[64,2,12,384]{3,0,2,1:T(8,128)(2,1)S(1)} %copy-done.9), kind=kOutput, calls=%fused_computation.14 | convolution fusion | flops 2417491968 | bytes 10616832 | tf_op jit(solution)/shard_map/slcd,slch->ldh/dot_general | solution.py:84
  401.8 7.9 %convert_reduce_fusion.1 = f32[64,24,1024]{2,1,0:T(8,128)} fusion(bf16[128,24,1024]{2,1,0:T(8,128)(2,1)} %all-to-all-done.1), kind=kLoop, calls=%fused_computation.7 | loop fusion | flops 4718592 | bytes 12582912 | tf_op jit(solution)/shard_map/reduce_sum | solution.py:62
  409.7 9.4 %gather_fusion.1 = f32[1024,1024]{1,0:T(8,128)} fusion(f32[1536,1024]{1,0:T(8,128)} %bitcast.140, s32[1024]{0:T(1024)S(1)} %broadcast_clamp_fusion), kind=kCustom, calls=%fused_computation.1 | custom fusion | bytes 8392704 | tf_op jit(solution)/shard_map/gather | solution.py:63
  423.6 41.6 %psum.7 = f32[128,8]{1,0:T(8,128)S(1)} all-reduce(f32[128,8]{1,0:T(8,128)S(1)} %get-tuple-element.12), channel_id=1, replica_groups=mesh['dp'=64,'col'=2] {'col'}, use_global_device_ids=true, to_apply=%region_9.10 | all-reduce | flops 1024 | bytes 8192 | tf_op jit(solution)/shard_map/psum | solution.py:95
  465.9 8.0 %convert_reduce_fusion = f32[64,24,1024]{2,1,0:T(8,128)} fusion(bf16[128,24,1024]{2,1,0:T(8,128)(2,1)} %all-to-all-done.3), kind=kLoop, calls=%fused_computation.6 | loop fusion | flops 4718592 | bytes 12582912 | tf_op jit(solution)/shard_map/reduce_sum | solution.py:62
  473.8 9.3 %gather_fusion.4 = f32[1024,1024]{1,0:T(8,128)} fusion(f32[1536,1024]{1,0:T(8,128)} %bitcast.139, s32[1024]{0:T(1024)S(1)} %broadcast_clamp_fusion), kind=kCustom, calls=%fused_computation.4 | custom fusion | bytes 8392704 | tf_op jit(solution)/shard_map/gather | solution.py:63
  (69 shorter events, 28.7 us)
Async XLA Ops:
  0.6 242.5 %copy-start = (bf16[2,384,2048]{2,1,0:T(8,128)(2,1)S(1)}, bf16[2,384,2048]{2,1,0:T(8,128)(2,1)}, u32[]{:S(2)}) copy-start(bf16[2,384,2048]{2,1,0:T(8,128)(2,1)} %param.12) | copy-start | bytes 9437188
  3.1 0.8 copy-start.8
  29.7 10.9 %copy-start.12 = (f32[128,8]{0,1:T(8,128)S(1)}, f32[128,8]{0,1:T(8,128)}, u32[]{:S(2)}) copy-start(f32[128,8]{0,1:T(8,128)} %param.9) | copy-start | bytes 12292
  29.7 96.0 %all-to-all-start = ((bf16[64,24,2048]{2,1,0:T(8,128)(2,1)}), bf16[64,24,2048]{2,1,0:T(8,128)(2,1)}, u32[]{:S(2)}, u32[]{:S(2)}) async-start(bf16[64,24,2048]{2,1,0:T(8,128)(2,1)} %broadcast_select_fusion), calls=%async_computation | async-start | bytes 12582912 | tf_op jit(solution)/shard_map/all_to_all | solution.py:37
  40.8 6.0 %copy-start.2 = (bf16[128,1024]{1,0:T(8,128)(2,1)S(1)}, bf16[128,1024]{1,0:T(8,128)(2,1)}, u32[]{:S(2)}) copy-start(bf16[128,1024]{1,0:T(8,128)(2,1)} %param.13) | copy-start | bytes 786436
  131.1 87.8 %all-to-all-start.2 = ((bf16[128,24,1024]{2,1,0:T(8,128)(2,1)}), bf16[128,24,1024]{2,1,0:T(8,128)(2,1)}, u32[]{:S(2)}, u32[]{:S(2)}) async-start(bf16[128,24,1024]{2,1,0:T(8,128)(2,1)} %bitcast.143), calls=%async_computation.2 | async-start | bytes 12582912 | tf_op jit(solution)/shard_map/all_to_all | solution.py:50
  140.2 6.4 %copy-start.6 = (bf16[2,2048,384]{2,1,0:T(8,128)(2,1)S(1)}, bf16[2,2048,384]{2,1,0:T(8,128)(2,1)}, u32[]{:S(2)}) copy-start(bf16[2,2048,384]{2,1,0:T(8,128)(2,1)} %param.11) | copy-start | bytes 9437188
  146.6 4.8 copy-start.3
  146.6 4.8 copy-start.4
  252.8 1.0 copy-start.13
  282.5 10.0 %copy-start.5 = (bf16[2,2048,384]{2,1,0:T(8,128)(2,1)S(1)}, bf16[2,2048,384]{2,1,0:T(8,128)(2,1)}, u32[]{:S(2)}) copy-start(bf16[2,2048,384]{2,1,0:T(8,128)(2,1)} %param.10) | copy-start | bytes 9437188
  282.5 88.8 %all-to-all-start.1 = ((bf16[128,24,1024]{2,1,0:T(8,128)(2,1)}), bf16[128,24,1024]{2,1,0:T(8,128)(2,1)}, u32[]{:S(2)}, u32[]{:S(2)}) async-start(bf16[128,24,1024]{2,1,0:T(8,128)(2,1)} %bitcast.142), calls=%async_computation.1 | async-start | bytes 12582912 | tf_op jit(solution)/shard_map/all_to_all | solution.py:60
  292.6 7.8 %copy-start.7 = (bf16[2,2048,384]{2,1,0:T(8,128)(2,1)S(1)}, bf16[2,2048,384]{2,1,0:T(8,128)(2,1)}, u32[]{:S(2)}) copy-start(bf16[2,2048,384]{2,1,0:T(8,128)(2,1)} %param.11) | copy-start | bytes 9437188
  292.6 7.8 %copy-start.10 = (bf16[64,2,12,384]{3,0,2,1:T(8,128)(2,1)S(1)}, bf16[64,2,12,384]{3,0,2,1:T(8,128)(2,1)}, u32[]{:S(2)}) copy-start(bf16[64,2,12,384]{3,0,2,1:T(8,128)(2,1)} %get-tuple-element.16) | copy-start | bytes 3538948
  371.3 10.1 %copy-start.14 = (bf16[64,2,12,384]{3,0,2,1:T(8,128)(2,1)S(1)}, bf16[64,2,12,384]{3,0,2,1:T(8,128)(2,1)}, u32[]{:S(2)}) copy-start(bf16[64,2,12,384]{3,0,2,1:T(8,128)(2,1)} %copy-done.13) | copy-start | bytes 3538948
  371.3 94.5 %all-to-all-start.3 = ((bf16[128,24,1024]{2,1,0:T(8,128)(2,1)}), bf16[128,24,1024]{2,1,0:T(8,128)(2,1)}, u32[]{:S(2)}, u32[]{:S(2)}) async-start(bf16[128,24,1024]{2,1,0:T(8,128)(2,1)} %bitcast.141), calls=%async_computation.3 | async-start | bytes 12582912 | tf_op jit(solution)/shard_map/all_to_all | solution.py:60
  381.5 7.3 %copy-start.11 = (bf16[64,2,12,384]{3,0,2,1:T(8,128)(2,1)S(1)}, bf16[64,2,12,384]{3,0,2,1:T(8,128)(2,1)}, u32[]{:S(2)}) copy-start(bf16[64,2,12,384]{3,0,2,1:T(8,128)(2,1)} %get-tuple-element.16) | copy-start | bytes 3538948
  381.5 15.3 %slice-start = ((s8[6291456]{0:T(1024)(128)(4,1)}), s8[4194304]{0:T(1024)(128)(4,1)S(1)}, s32[]{:S(2)}) async-start(s8[6291456]{0:T(1024)(128)(4,1)} %bitcast.152), calls=%async_computation.4 | async-start | bytes 8388608
  388.7 8.1 %slice-start.1 = ((s8[6291456]{0:T(1024)(128)(4,1)}), s8[2097152]{0:T(1024)(128)(4,1)S(1)}, s32[]{:S(2)}) async-start(s8[6291456]{0:T(1024)(128)(4,1)} %bitcast.152), calls=%async_computation.5 | async-start | bytes 4194304
  388.7 8.1 %copy-start.9 = (bf16[64,2,12,384]{3,0,2,1:T(8,128)(2,1)S(1)}, bf16[64,2,12,384]{3,0,2,1:T(8,128)(2,1)}, u32[]{:S(2)}) copy-start(bf16[64,2,12,384]{3,0,2,1:T(8,128)(2,1)} %get-tuple-element.17) | copy-start | bytes 3538948
  473.8 13.3 %copy-start.1 = (bf16[2,384,2048]{2,1,0:T(8,128)(2,1)S(1)}, bf16[2,384,2048]{2,1,0:T(8,128)(2,1)}, u32[]{:S(2)}) copy-start(bf16[2,384,2048]{2,1,0:T(8,128)(2,1)} %param.12) | copy-start | bytes 9437188

commit v2 on v1

--- a/solution.py
+++ b/solution.py
@@ -24,25 +24,27 @@
     slot_index = jnp.sum(before * onehot, axis=1)
     flat_index = flat_routes * slot_cap + slot_index
 
-    pair_of_slot = jnp.full((slots,), pair_count, jnp.int32).at[flat_index].set(
-        jnp.arange(pair_count, dtype=jnp.int32)
-    )
-    valid = pair_of_slot < pair_count
-    safe_pair = jnp.where(valid, pair_of_slot, 0)
-    token_of_slot = safe_pair // top_count
+    slot_ids = jnp.arange(slots, dtype=jnp.int32)
+    match = flat_index.reshape(tok_count, top_count)[:, :, None] == slot_ids[None, None, :]
+    weight = jnp.sum(jnp.where(match, probs[:, :, None], 0.0), axis=1)
+    taken = jnp.any(match, axis=1)
+    picker = taken.astype(jnp.bfloat16)
+    weight_hi = weight.astype(jnp.bfloat16)
+    weight_lo = (weight - weight_hi.astype(jnp.float32)).astype(jnp.bfloat16)
+    prob_of_slot = jnp.sum(weight, axis=0)
 
     both = ("dp", "col")
 
-    send_tok = jnp.where(valid[:, None], tokens[token_of_slot], jnp.zeros((), tokens.dtype))
+    send_tok = jnp.einsum(
+        "ts,td->sd", picker, tokens, preferred_element_type=jnp.float32
+    ).astype(jnp.bfloat16)
     arrived_rows = lax.all_to_all(
         send_tok.reshape(owners, rows_per_owner, width), "dp", 0, 0, tiled=True
     )
     row_block = arrived_rows.reshape(owners, local_experts, slot_cap, width)
 
-    prob_of_slot = jnp.where(valid, probs.reshape(-1)[safe_pair], 0.0)
-    send_cot = (prob_of_slot[:, None] * cotangent[token_of_slot].astype(jnp.float32)).astype(
-        jnp.bfloat16
-    )
+    cot_rows = jnp.einsum("ts,td->sd", picker, cotangent, preferred_element_type=jnp.float32)
+    send_cot = (prob_of_slot[:, None] * cot_rows).astype(jnp.bfloat16)
     send_cot = jnp.broadcast_to(
         send_cot.reshape(owners, 1, rows_per_owner, half_width),
         (owners, cols, rows_per_owner, half_width),
@@ -54,13 +56,20 @@
         .reshape(owners, local_experts, slot_cap, width)
     )
 
+    def per_half(table):
+        return jnp.broadcast_to(
+            table.reshape(tok_count, owners, 1, rows_per_owner),
+            (tok_count, owners, cols, rows_per_owner),
+        )
+
     def send_back(partial_value):
         part = partial_value.astype(jnp.bfloat16).reshape(owners, rows_per_owner, cols, half_width)
         part = part.transpose(0, 2, 1, 3).reshape(owners * cols, rows_per_owner, half_width)
         got = lax.all_to_all(part, both, 0, 0, tiled=True)
-        got = got.reshape(owners, cols, rows_per_owner, half_width).astype(jnp.float32)
-        summed = jnp.sum(got, axis=1).reshape(slots, half_width)
-        return summed[flat_index].reshape(tok_count, top_count, half_width)
+        return got.reshape(owners, cols, rows_per_owner, half_width)
+
+    def combine(table, got):
+        return jnp.einsum("tocr,ocrd->td", per_half(table), got, preferred_element_type=jnp.float32)
 
     gate_acts = jnp.einsum("slcd,ldh->slch", row_block, w_gate, preferred_element_type=jnp.float32)
     up_acts = jnp.einsum("slcd,ldh->slch", row_block, w_up, preferred_element_type=jnp.float32)
@@ -68,10 +77,11 @@
     silu_g = gate_acts * sigmoid_g
     hidden = (silu_g * up_acts).astype(jnp.bfloat16)
     out_partial = jnp.einsum("slch,lhd->slcd", hidden, w_down, preferred_element_type=jnp.float32)
-    picked_wide = send_back(out_partial)
-    mixed = jnp.sum(probs[:, :, None] * picked_wide, axis=1).astype(jnp.bfloat16)
-    cot_wide = cotangent.astype(jnp.float32)
-    prob_part = jnp.sum(cot_wide[:, None, :] * picked_wide, axis=2)
+    got_out = send_back(out_partial)
+    mixed = (combine(weight_hi, got_out) + combine(weight_lo, got_out)).astype(jnp.bfloat16)
+    dots = jnp.einsum("td,ocrd->tocr", cotangent, got_out, preferred_element_type=jnp.float32)
+    dots = jnp.sum(dots, axis=2).reshape(tok_count, 1, slots)
+    prob_part = jnp.sum(jnp.where(match, dots, 0.0), axis=2)
 
     grad_down = jnp.einsum(
         "slch,slcd->lhd", hidden, d_out, preferred_element_type=jnp.float32
@@ -90,9 +100,9 @@
     d_partial = jnp.einsum(
         "slch,ldh->slcd", d_gate, w_gate, preferred_element_type=jnp.float32
     ) + jnp.einsum("slch,ldh->slcd", d_up, w_up, preferred_element_type=jnp.float32)
-    picked_grad = send_back(d_partial)
-    grad_tokens = jnp.sum(picked_grad, axis=1).astype(jnp.bfloat16)
-    grad_probs = lax.psum(prob_part, "col")
+    got_grad = send_back(d_partial)
+    grad_tokens = combine(picker, got_grad).astype(jnp.bfloat16)
+    grad_probs = prob_part + lax.ppermute(prob_part, "col", perm=[(0, 1), (1, 0)])
     return (mixed, grad_tokens, grad_probs, grad_gate, grad_up, grad_down)
 
 

time: 495 us -> 521 us (1.053)
  blocking collectives: 41.6 us -> 163 us
  local copies, waits for them, and re-layouts: 135 us -> 84.1 us
  matrix products: 60.8 us -> 94.3 us
  waiting for transfers between devices: 171 us -> 140 us
  other arithmetic: 37 us -> 9.87 us
  starting transfers between devices: 40 us -> 21.6 us
    all_to_all x0 -> x2, blocking collectives: none -> 163 us  [the longest x1 82.8 us: body(): lax.all_to_all(send_tok.reshape(owners, rows_per_owner, width), 'dp', 0,...]
    all_to_all x2 -> x0, waiting for transfers between devices: 132 us -> none  [the longest x1 69 us: body(): lax.all_to_all(send_tok.reshape(owners, rows_per_owner, width), 'dp', 0,...]
    ppermute x0 -> x1, waiting for transfers between devices: none -> 59.1 us  [body(): lax.ppermute(prob_part, 'col', perm=[(0, 1), (1, 0)])]
    gather x5 -> x0, local copies, waits for them, and re-layouts: 44.2 us -> none  [the longest x2 18.7 us: send_back(): return summed[flat_index].reshape(tok_count, top_count, half_width)]
    dot_general x0 -> x6, matrix products: none -> 42.2 us  [the longest x3 31.3 us: combine(): jnp.einsum('tocr,ocrd->td', per_half(table), got, preferred_element_type=...]
    psum x1 -> x0, blocking collectives: 41.6 us -> none  [body(): grad_probs = lax.psum(prob_part, 'col')]
    all_to_all x2, waiting for transfers between devices: 39.6 us -> 80.8 us  [send_back(): got = lax.all_to_all(part, both, 0, 0, tiled=True)]
    all_to_all x2 -> x0, starting transfers between devices: 19.9 us -> none  [the longest x1 10.9 us: body(): lax.all_to_all(send_tok.reshape(owners, rows_per_owner, width), 'dp', 0,...]
  transfers between devices with their start and end apart: 4 -> 3, of which waited for: 3 -> 2; matrix products, arithmetic and copies ran while one was open for 23% -> 8% of each run, Pallas kernels for 0% -> 0%
where the time goes in v2:
time: 521 us; the launch traced here: 514 us
  blocking collectives  163 us (31%)
  waiting for transfers between devices  140 us (27%)
  matrix products  94.3 us (18%)
  local copies, waits for them, and re-layouts  84.1 us (16%)
  starting transfers between devices  21.6 us (4%)
  other arithmetic  9.87 us (2%)
    all_to_all x1, blocking collectives, body(): lax.all_to_all(send_tok.reshape(owners, rows_per_owner, width), 'dp', 0,...  82.8 us
    all_to_all x2, waiting for transfers between devices, send_back(): got = lax.all_to_all(part, both, 0, 0, tiled=True)  80.8 us
    all_to_all x1, blocking collectives, body(): arrived_cot = lax.all_to_all(send_cot, both, 0, 0, tiled=True)  79.9 us
    ppermute x1, waiting for transfers between devices, body(): lax.ppermute(prob_part, 'col', perm=[(0, 1), (1, 0)])  59.1 us
    dot_general x3, matrix products, combine(): jnp.einsum('tocr,ocrd->td', per_half(table), got, preferred_element_type=...  31.3 us
    transpose x2, local copies, waits for them, and re-layouts, send_back(): part.transpose(0, 2, 1, 3)  24.2 us
    reshape x2, local copies, waits for them, and re-layouts, send_back(): partial_value.astype(jnp.bfloat16)  22.8 us
    all_to_all x2, starting transfers between devices, send_back(): got = lax.all_to_all(part, both, 0, 0, tiled=True)  20.2 us
  transfers between devices with their start and end apart: 3, of which 2 were waited for; matrix products, arithmetic and copies ran while one was open for 8% of the time, Pallas kernels for 0%

profile of v2, /device:TPU:82, one launch (start us, length us, event | category | flops | bytes accessed | tf_op | source)
XLA Modules:
  0.0 513.7 jit_solution(11376279825354309712)
XLA Ops:
  4.8 3.2 fusion.3
  7.9 2.9 convolution_convert_fusion
  10.8 82.8 %all_to_all.20 = bf16[64,24,2048]{2,1,0:T(8,128)(2,1)S(1)} all-to-all(bf16[64,24,2048]{2,1,0:T(8,128)(2,1)S(1)} %bitcast.155), channel_id=1, replica_groups=mesh['dp'=64,'col'=2] {'dp'}, dimensions={0} | all-to-all | bytes 12582912 | tf_op jit(solution)/shard_map/all_to_all | solution.py:41
  93.6 3.4 copy.84
  97.1 3.4 fusion.13
  101.2 4.8 fusion.22
  107.1 5.3 %convert_bitcast_fusion = bf16[64,2,12,2048]{3,0,2,1:T(8,128)(2,1)} fusion(bf16[64,2,12,384]{3,0,2,1:T(8,128)(2,1)S(1)} %get-tuple-element.25, bf16[2,384,2048]{2,1,0:T(8,128)(2,1)S(1)} %copy-done), kind=kOutput, calls=%fused_computation.13 | convolution fusion | flops 2419064832 | bytes 10616832 | tf_op jit(solution)/shard_map/slch,lhd->slcd/dot_general | solution.py:79
  112.4 11.3 %reshape.102 = bf16[64,24,2,1024]{3,2,0,1:T(2,128)(2,1)} reshape(bf16[64,2,12,2048]{3,0,2,1:T(8,128)(2,1)} %convert_bitcast_fusion) | data formatting | bytes 12582912 | tf_op jit(solution)/shard_map/reshape | solution.py:66
  123.7 12.1 %copy.85 = bf16[64,2,24,1024]{3,2,1,0:T(8,128)(2,1)} copy(bf16[64,2,24,1024]{3,1,0,2:T(2,128)(2,1)} %bitcast.158) | data formatting | bytes 12582912 | tf_op jit(solution)/shard_map/transpose | solution.py:67
  135.8 9.4 %all-to-all-start.1 = ((bf16[128,24,1024]{2,1,0:T(8,128)(2,1)}), bf16[128,24,1024]{2,1,0:T(8,128)(2,1)}, u32[]{:S(2)}, u32[]{:S(2)}) async-start(bf16[128,24,1024]{2,1,0:T(8,128)(2,1)} %bitcast.157), calls=%async_computation.1 | async-start | bytes 12582912 | tf_op jit(solution)/shard_map/all_to_all | solution.py:68
  145.3 80.8 %all-to-all-done.1 = bf16[128,24,1024]{2,1,0:T(8,128)(2,1)} async-done(((bf16[128,24,1024]{2,1,0:T(8,128)(2,1)}), bf16[128,24,1024]{2,1,0:T(8,128)(2,1)}, u32[]{:S(2)}, u32[]{:S(2)}) %all-to-all-start.1) | async-done | bytes 6291488 | tf_op jit(solution)/shard_map/all_to_all | solution.py:68
  226.0 6.0 %convolution_reduce_fusion = f32[64,24,128]{2,1,0:T(8,128)} fusion(bf16[64,2,24,1024]{3,2,1,0:T(8,128)(2,1)} %bitcast.17, bf16[128,1024]{1,0:T(8,128)(2,1)} %param.13), kind=kOutput, calls=%fused_computation.45 | convolution fusion | flops 805502976 | bytes 7340032 | tf_op jit(solution)/shard_map/td,ocrd->tocr/dot_general | solution.py:82
  232.0 2.3 copy.94
  234.4 4.9 select_reduce_fusion
  239.3 2.0 multiply_convert_fusion
  242.2 79.9 %all_to_all.21 = bf16[128,24,1024]{2,1,0:T(8,128)(2,1)S(1)} all-to-all(bf16[128,24,1024]{2,1,0:T(8,128)(2,1)S(1)} %bitcast.159), channel_id=1, replica_groups=mesh['dp'=64,'col'=2] {'dp','col'}, dimensions={0} | all-to-all | bytes 12582912 | tf_op jit(solution)/shard_map/all_to_all | solution.py:52
  322.1 13.7 %copy.125 = bf16[64,2,24,1024]{3,1,0,2:T(2,128)(2,1)} copy(bf16[64,2,24,1024]{3,2,1,0:T(8,128)(2,1)S(1)} %bitcast.160) | data formatting | bytes 12582912 | tf_op jit(solution)/shard_map/reshape | solution.py:54
  335.8 11.1 %reshape.107 = bf16[64,2,12,2048]{3,0,2,1:T(8,128)(2,1)} reshape(bf16[64,24,2,1024]{3,2,0,1:T(2,128)(2,1)} %bitcast.161) | data formatting | bytes 12582912 | tf_op jit(solution)/shard_map/reshape | solution.py:56
  346.9 9.4 %fusion.21 = (bf16[64,2,12,384]{3,0,2,1:T(8,128)(2,1)}, bf16[64,2,12,384]{3,0,2,1:T(8,128)(2,1)S(1)}) fusion(f32[2,64,12,384]{3,1,2,0:T(8,128)} %copy-done.15, f32[2,64,12,384]{3,1,2,0:T(8,128)} %get-tuple-element.26, bf16[64,2,12,2048]{3,0,2,1:T(8,128)(2,1)} %reshape.107, bf16[2,384,2048]{2,1,0:T(8,128)(2,1)S(1)} %copy-done), kind=kOutput, calls=%fused_computation.35 | convolution fusion | flops 2423586816 | bytes 16515072 | tf_op jit(solution)/shard_map/slcd,lhd->slch/dot_general | solution.py:89
  356.4 3.4 fusion.11
  359.8 8.3 %fusion = bf16[64,2,12,2048]{3,0,2,1:T(8,128)(2,1)} fusion(f32[2,64,12,2048]{3,1,2,0:T(8,128)S(1)} %fusion.11, bf16[64,2,12,384]{3,0,2,1:T(8,128)(2,1)} %get-tuple-element.23, bf16[2,2048,384]{2,1,0:T(8,128)(2,1)} %param.11), kind=kOutput, calls=%fused_computation.4 | convolution fusion | flops 2422210560 | bytes 23199744 | tf_op jit(solution)/shard_map/slch,ldh->slcd/dot_general | solution.py:102
  368.1 11.5 %reshape.108 = bf16[64,24,2,1024]{3,2,0,1:T(2,128)(2,1)} reshape(bf16[64,2,12,2048]{3,0,2,1:T(8,128)(2,1)} %fusion) | data formatting | bytes 12582912 | tf_op jit(solution)/shard_map/reshape | solution.py:66
  379.7 12.1 %copy.92 = bf16[64,2,24,1024]{3,2,1,0:T(8,128)(2,1)} copy(bf16[64,2,24,1024]{3,1,0,2:T(2,128)(2,1)} %bitcast.162) | data formatting | bytes 12582912 | tf_op jit(solution)/shard_map/transpose | solution.py:67
  391.8 10.8 %all-to-all-start.3 = ((bf16[128,24,1024]{2,1,0:T(8,128)(2,1)}), bf16[128,24,1024]{2,1,0:T(8,128)(2,1)}, u32[]{:S(2)}, u32[]{:S(2)}) async-start(bf16[128,24,1024]{2,1,0:T(8,128)(2,1)} %bitcast.156), calls=%async_computation.3 | async-start | bytes 12582912 | tf_op jit(solution)/shard_map/all_to_all | solution.py:68
  402.9 1.5 collective-permute-start
  405.0 9.8 %fusion.27 = f32[128,1024]{1,0:T(8,128)S(1)} fusion(bf16[64,2,24,1024]{3,2,1,0:T(8,128)(2,1)} %bitcast.17, bf16[128,64,24]{0,1,2:T(8,128)(2,1)S(1)} %copy.83), kind=kOutput, calls=%fused_computation.46 | convolution fusion | flops 805306368 | bytes 7208960 | tf_op jit(solution)/shard_map/tocr,ocrd->td/dot_general | solution.py:72
  414.8 10.9 %fusion.39 = bf16[128,1024]{1,0:T(8,128)(2,1)} fusion(f32[128,1024]{1,0:T(8,128)S(1)} %fusion.27, bf16[64,2,24,1024]{3,2,1,0:T(8,128)(2,1)} %bitcast.17, bf16[128,64,24]{0,1,2:T(8,128)(2,1)S(1)} %copy.87), kind=kOutput, calls=%fused_computation.50 | convolution fusion | flops 805568512 | bytes 7471104 | tf_op jit(solution)/shard_map/tocr,ocrd->td/dot_general | solution.py:72
  425.6 59.1 %collective-permute-done = f32[128,8]{1,0:T(8,128)S(1)} collective-permute-done((f32[128,8]{1,0:T(8,128)S(1)}, f32[128,8]{1,0:T(8,128)S(1)}, u32[]{:S(2)}, u32[]{:S(2)}) %collective-permute-start) | collective-permute-done | bytes 4128 | tf_op jit(solution)/shard_map/ppermute | solution.py:105
  485.4 7.6 %bitcast_convert_fusion = bf16[2,384,2048]{2,1,0:T(8,128)(2,1)} fusion(bf16[64,2,12,384]{3,0,2,1:T(8,128)(2,1)} %copy-done.14, bf16[64,2,12,2048]{3,0,2,1:T(8,128)(2,1)} %reshape.107), kind=kOutput, calls=%fused_computation.5 | convolution fusion | flops 2417491968 | bytes 10616832 | tf_op jit(solution)/shard_map/slch,slcd->lhd/dot_general | solution.py:86
  493.0 4.9 bitcast_convert_fusion.1
  497.9 4.9 bitcast_convert_fusion.2
  502.8 10.7 %fusion.42 = bf16[128,1024]{1,0:T(8,128)(2,1)} fusion(bf16[64,2,24,1024]{3,2,1,0:T(8,128)(2,1)} %bitcast.34, bf16[128,64,24]{0,1,2:T(8,128)(2,1)S(1)} %copy.90), kind=kOutput, calls=%fused_computation.51 | convolution fusion | flops 805437440 | bytes 6946816 | tf_op jit(solution)/shard_map/tocr,ocrd->td/dot_general | solution.py:72
  (64 shorter events, 8.4 us)
Async XLA Ops:
  0.6 106.5 %copy-start = (bf16[2,384,2048]{2,1,0:T(8,128)(2,1)S(1)}, bf16[2,384,2048]{2,1,0:T(8,128)(2,1)}, u32[]{:S(2)}) copy-start(bf16[2,384,2048]{2,1,0:T(8,128)(2,1)} %param.12) | copy-start | bytes 9437188
  0.6 4.0 copy-start.12
  2.1 0.8 copy-start.7
  93.6 3.5 copy-start.3
  97.1 3.4 copy-start.2
  97.1 4.2 copy-start.6
  101.2 4.8 copy-start.15
  106.1 1.0 copy-start.14
  135.8 9.4 %copy-start.13 = (f32[128,8]{0,1:T(8,128)S(1)}, f32[128,8]{0,1:T(8,128)}, u32[]{:S(2)}) copy-start(f32[128,8]{0,1:T(8,128)} %param.9) | copy-start | bytes 12292
  135.8 90.3 %all-to-all-start.1 = ((bf16[128,24,1024]{2,1,0:T(8,128)(2,1)}), bf16[128,24,1024]{2,1,0:T(8,128)(2,1)}, u32[]{:S(2)}, u32[]{:S(2)}) async-start(bf16[128,24,1024]{2,1,0:T(8,128)(2,1)} %bitcast.157), calls=%async_computation.1 | async-start | bytes 12582912 | tf_op jit(solution)/shard_map/all_to_all | solution.py:68
  346.9 9.5 %copy-start.4 = (bf16[2,2048,384]{2,1,0:T(8,128)(2,1)S(1)}, bf16[2,2048,384]{2,1,0:T(8,128)(2,1)}, u32[]{:S(2)}) copy-start(bf16[2,2048,384]{2,1,0:T(8,128)(2,1)} %param.10) | copy-start | bytes 9437188
  356.4 3.5 copy-start.8
  391.8 11.1 %copy-start.11 = (f32[128,8]{1,0:T(8,128)S(1)}, f32[128,8]{1,0:T(8,128)}, u32[]{:S(2)}) copy-start(f32[128,8]{1,0:T(8,128)} %get-tuple-element.20) | copy-start | bytes 12292
  391.8 12.6 %copy-start.5 = (f32[128,1536]{1,0:T(8,128)S(1)}, f32[128,1536]{1,0:T(8,128)}, u32[]{:S(2)}) copy-start(f32[128,1536]{1,0:T(8,128)} %get-tuple-element.19) | copy-start | bytes 2359300
  391.8 111.0 %all-to-all-start.3 = ((bf16[128,24,1024]{2,1,0:T(8,128)(2,1)}), bf16[128,24,1024]{2,1,0:T(8,128)(2,1)}, u32[]{:S(2)}, u32[]{:S(2)}) async-start(bf16[128,24,1024]{2,1,0:T(8,128)(2,1)} %bitcast.156), calls=%async_computation.3 | async-start | bytes 12582912 | tf_op jit(solution)/shard_map/all_to_all | solution.py:68
  402.9 81.8 %collective-permute-start = (f32[128,8]{1,0:T(8,128)S(1)}, f32[128,8]{1,0:T(8,128)S(1)}, u32[]{:S(2)}, u32[]{:S(2)}) collective-permute-start(f32[128,8]{1,0:T(8,128)S(1)} %copy-done.11), channel_id=1, source_target_pairs={{0,1},{1,0},{2,3},{3,2},{4,5},{5,4},{6,7},{7,6},{8,9},{9,8},{10,11... | collective-permute-start | bytes 12296 | tf_op jit(solution)/shard_map/ppermute | solution.py:105
  414.8 78.2 %slice-start = ((s8[6291456]{0:T(1024)(128)(4,1)}), s8[2097152]{0:T(1024)(128)(4,1)S(1)}, s32[]{:S(2)}) async-start(s8[6291456]{0:T(1024)(128)(4,1)} %bitcast.166), calls=%async_computation.4 | async-start | bytes 4194304
  485.4 7.6 %slice-start.1 = ((s8[6291456]{0:T(1024)(128)(4,1)}), s8[4194304]{0:T(1024)(128)(4,1)S(1)}, s32[]{:S(2)}) async-start(s8[6291456]{0:T(1024)(128)(4,1)} %bitcast.166), calls=%async_computation.5 | async-start | bytes 8388608
  485.4 7.6 %copy-start.10 = (bf16[64,2,12,384]{3,0,2,1:T(8,128)(2,1)S(1)}, bf16[64,2,12,384]{3,0,2,1:T(8,128)(2,1)}, u32[]{:S(2)}) copy-start(bf16[64,2,12,384]{3,0,2,1:T(8,128)(2,1)} %get-tuple-element.23) | copy-start | bytes 3538948
  493.0 4.9 copy-start.9
  502.8 10.7 %copy-start.1 = (bf16[2,384,2048]{2,1,0:T(8,128)(2,1)S(1)}, bf16[2,384,2048]{2,1,0:T(8,128)(2,1)}, u32[]{:S(2)}) copy-start(bf16[2,384,2048]{2,1,0:T(8,128)(2,1)} %param.12) | copy-start | bytes 9437188

commit v3 on v2

--- a/solution.py
+++ b/solution.py
@@ -50,6 +50,8 @@
         (owners, cols, rows_per_owner, half_width),
     ).reshape(owners * cols, rows_per_owner, half_width)
     arrived_cot = lax.all_to_all(send_cot, both, 0, 0, tiled=True)
+    arrived_rows, arrived_cot = lax.optimization_barrier((arrived_rows, arrived_cot))
+    row_block = arrived_rows.reshape(owners, local_experts, slot_cap, width)
     d_out = (
         arrived_cot.reshape(owners, cols, rows_per_owner, half_width)
         .transpose(0, 2, 1, 3)
@@ -100,9 +102,11 @@
     d_partial = jnp.einsum(
         "slch,ldh->slcd", d_gate, w_gate, preferred_element_type=jnp.float32
     ) + jnp.einsum("slch,ldh->slcd", d_up, w_up, preferred_element_type=jnp.float32)
+    prob_other = lax.ppermute(prob_part, "col", perm=[(0, 1), (1, 0)])
+    prob_other, d_partial = lax.optimization_barrier((prob_other, d_partial))
     got_grad = send_back(d_partial)
     grad_tokens = combine(picker, got_grad).astype(jnp.bfloat16)
-    grad_probs = prob_part + lax.ppermute(prob_part, "col", perm=[(0, 1), (1, 0)])
+    grad_probs = prob_part + prob_other
     return (mixed, grad_tokens, grad_probs, grad_gate, grad_up, grad_down)
 
 

time: 521 us -> 518 us (level)
  the two profiles are of different devices: /device:TPU:82 before, /device:TPU:98 now
where the time goes in v3:
time: 518 us; the launch traced here: 510 us
  waiting for transfers between devices  193 us (37%)
  matrix products  103 us (20%)
  local copies, waits for them, and re-layouts  89.3 us (17%)
  blocking collectives  87.5 us (17%)
  starting transfers between devices  26.4 us (5%)
  other arithmetic  9.22 us (2%)
    all_to_all x2, waiting for transfers between devices, send_back(): got = lax.all_to_all(part, both, 0, 0, tiled=True)  121 us
    all_to_all x1, blocking collectives, body(): arrived_cot = lax.all_to_all(send_cot, both, 0, 0, tiled=True)  87.5 us
    all_to_all x1, waiting for transfers between devices, body(): lax.all_to_all(send_tok.reshape(owners, rows_per_owner, width), 'dp', 0,...  72.4 us
    dot_general x3, matrix products, combine(): jnp.einsum('tocr,ocrd->td', per_half(table), got, preferred_element_type=...  31.2 us
    transpose x2, local copies, waits for them, and re-layouts, send_back(): part.transpose(0, 2, 1, 3)  24.4 us
    reshape x2, local copies, waits for them, and re-layouts, send_back(): partial_value.astype(jnp.bfloat16)  22.5 us
    all_to_all x2, starting transfers between devices, send_back(): got = lax.all_to_all(part, both, 0, 0, tiled=True)  15.9 us
    transpose x1, local copies, waits for them, and re-layouts, body(): d_out = arrived_cot.reshape(owners, cols, rows_per_owner, half_width).tra...  13.6 us
  transfers between devices with their start and end apart: 4, of which 3 were waited for; matrix products, arithmetic and copies ran while one was open for 13% of the time, Pallas kernels for 0%

profile of v3, /device:TPU:98, one launch (start us, length us, event | category | flops | bytes accessed | tf_op | source)
XLA Modules:
  0.0 509.6 jit_solution(6948737153909190655)
XLA Ops:
  4.8 3.2 fusion.2
  7.9 5.5 %convolution_convert_fusion = bf16[1536,2048]{1,0:T(8,128)(2,1)} fusion(pred[128,1536]{1,0:T(8,128)(4,1)S(1)} %fusion.2, bf16[128,2048]{1,0:T(8,128)(2,1)} %param.7), kind=kOutput, calls=%fused_computation.3 | convolution fusion | flops 808452096 | bytes 7012352 | tf_op jit(solution)/shard_map/ts,td->sd/dot_general | solution.py:38
  13.5 10.5 %all-to-all-start = ((bf16[64,24,2048]{2,1,0:T(8,128)(2,1)}), bf16[64,24,2048]{2,1,0:T(8,128)(2,1)}, u32[]{:S(2)}, u32[]{:S(2)}) async-start(bf16[64,24,2048]{2,1,0:T(8,128)(2,1)} %bitcast.152), calls=%async_computation | async-start | bytes 12582912 | tf_op jit(solution)/shard_map/all_to_all | solution.py:41
  24.1 3.3 select_reduce_fusion.1
  27.4 3.7 multiply_convert_fusion
  31.0 72.4 %all-to-all-done = bf16[64,24,2048]{2,1,0:T(8,128)(2,1)} async-done(((bf16[64,24,2048]{2,1,0:T(8,128)(2,1)}), bf16[64,24,2048]{2,1,0:T(8,128)(2,1)}, u32[]{:S(2)}, u32[]{:S(2)}) %all-to-all-start) | async-done | bytes 6291488 | tf_op jit(solution)/shard_map/all_to_all | solution.py:41
  103.5 2.7 broadcast_in_dim.54
  106.2 87.5 %all_to_all.20 = bf16[128,24,1024]{2,1,0:T(8,128)(2,1)S(1)} all-to-all(bf16[128,24,1024]{2,1,0:T(8,128)(2,1)S(1)} %bitcast.156), channel_id=1, replica_groups=mesh['dp'=64,'col'=2] {'dp','col'}, dimensions={0} | all-to-all | bytes 12582912 | tf_op jit(solution)/shard_map/all_to_all | solution.py:52
  193.6 8.8 %copy.84 = bf16[64,24,2048]{2,0,1:T(8,128)(2,1)} copy(bf16[64,24,2048]{2,1,0:T(8,128)(2,1)} %all-to-all-done) | data formatting | bytes 12582912 | tf_op jit(solution)/shard_map/optimization_barrier | solution.py:53
  202.5 13.6 %copy.92 = bf16[64,24,2,1024]{3,2,0,1:T(2,128)(2,1)} copy(bf16[64,24,2,1024]{3,1,2,0:T(8,128)(2,1)S(1)} %bitcast.155) | data formatting | bytes 12582912 | tf_op jit(solution)/shard_map/transpose | solution.py:57
  216.1 11.2 %reshape.107 = bf16[64,2,12,2048]{3,0,2,1:T(8,128)(2,1)} reshape(bf16[64,24,2,1024]{3,2,0,1:T(2,128)(2,1)} %copy.92) | data formatting | bytes 12582912 | tf_op jit(solution)/shard_map/reshape | solution.py:58
  227.2 6.6 %fusion.8 = f32[2,64,12,384]{3,1,2,0:T(8,128)S(1)} fusion(bf16[64,2,12,2048]{3,0,2,1:T(8,128)(2,1)} %bitcast.160, bf16[2,2048,384]{2,1,0:T(8,128)(2,1)} %param.11), kind=kOutput, calls=%fused_computation.19 | convolution fusion | flops 2415919104 | bytes 11796480 | tf_op jit(solution)/shard_map/slcd,ldh->slch/dot_general | solution.py:77
  233.8 5.7 %fusion.12 = f32[2,64,12,384]{3,1,2,0:T(8,128)S(1)} fusion(bf16[64,2,12,2048]{3,0,2,1:T(8,128)(2,1)} %bitcast.161, bf16[2,2048,384]{2,1,0:T(8,128)(2,1)S(1)} %copy-done.2), kind=kOutput, calls=%fused_computation.23 | convolution fusion | flops 2415919104 | bytes 11796480 | tf_op jit(solution)/shard_map/slcd,ldh->slch/dot_general | solution.py:76
  239.6 5.4 %fusion.20 = (bf16[64,2,12,384]{3,0,2,1:T(8,128)(2,1)}, bf16[64,2,12,384]{3,0,2,1:T(8,128)(2,1)}, bf16[64,2,12,384]{3,0,2,1:T(8,128)(2,1)S(1)}) fusion(f32[2,64,12,384]{3,1,2,0:T(8,128)S(1)} %fusion.12, f32[2,64,12,384]{3,1,2,0:T(8,128)S(1)} %fusion.8, bf16[64,2,12,2048]{3,0,2,1:T(8,128)(2,1)S(1)} %bitcast.167, bf16[2,384,2048]{2,1,0:T(8,128)(2,1)S(1)} %copy-done), kind=kOutput, calls=%fused_computation.33 | convolution fusion | flops 2424766464 | bytes 17694720 | tf_op jit(solution)/shard_map/slcd,lhd->slch/dot_general | solution.py:91
  246.0 5.3 %convert_bitcast_fusion = bf16[64,2,12,2048]{3,0,2,1:T(8,128)(2,1)} fusion(bf16[64,2,12,384]{3,0,2,1:T(8,128)(2,1)S(1)} %get-tuple-element.32, bf16[2,384,2048]{2,1,0:T(8,128)(2,1)S(1)} %copy-done), kind=kOutput, calls=%fused_computation.10 | convolution fusion | flops 2419064832 | bytes 10616832 | tf_op jit(solution)/shard_map/slch,lhd->slcd/dot_general | solution.py:81
  251.3 11.3 %reshape.103 = bf16[64,24,2,1024]{3,2,0,1:T(2,128)(2,1)} reshape(bf16[64,2,12,2048]{3,0,2,1:T(8,128)(2,1)} %convert_bitcast_fusion) | data formatting | bytes 12582912 | tf_op jit(solution)/shard_map/reshape | solution.py:68
  262.6 12.2 %copy.85 = bf16[64,2,24,1024]{3,2,1,0:T(8,128)(2,1)} copy(bf16[64,2,24,1024]{3,1,0,2:T(2,128)(2,1)} %bitcast.157) | data formatting | bytes 12582912 | tf_op jit(solution)/shard_map/transpose | solution.py:69
  274.8 8.4 %all-to-all-start.2 = ((bf16[128,24,1024]{2,1,0:T(8,128)(2,1)}), bf16[128,24,1024]{2,1,0:T(8,128)(2,1)}, u32[]{:S(2)}, u32[]{:S(2)}) async-start(bf16[128,24,1024]{2,1,0:T(8,128)(2,1)} %bitcast.154), calls=%async_computation.2 | async-start | bytes 12582912 | tf_op jit(solution)/shard_map/all_to_all | solution.py:70
  283.2 7.7 %fusion.10 = f32[2,64,12,2048]{3,1,2,0:T(8,128)} fusion(bf16[64,2,12,384]{3,0,2,1:T(8,128)(2,1)} %get-tuple-element.31, bf16[2,2048,384]{2,1,0:T(8,128)(2,1)S(1)} %copy-done.3), kind=kOutput, calls=%fused_computation.21 | convolution fusion | flops 2415919104 | bytes 16908288 | tf_op jit(solution)/shard_map/slch,ldh->slcd/dot_general | solution.py:102
  290.9 76.8 %all-to-all-done.2 = bf16[128,24,1024]{2,1,0:T(8,128)(2,1)} async-done(((bf16[128,24,1024]{2,1,0:T(8,128)(2,1)}), bf16[128,24,1024]{2,1,0:T(8,128)(2,1)}, u32[]{:S(2)}, u32[]{:S(2)}) %all-to-all-start.2) | async-done | bytes 6291488 | tf_op jit(solution)/shard_map/all_to_all | solution.py:70
  367.6 4.7 convolution_reduce_fusion
  373.7 9.7 %add_bitcast_fusion = bf16[64,2,12,2048]{3,0,2,1:T(8,128)(2,1)} fusion(f32[2,64,12,2048]{3,1,2,0:T(8,128)} %fusion.10, bf16[64,2,12,384]{3,0,2,1:T(8,128)(2,1)S(1)} %copy-done.7, bf16[2,2048,384]{2,1,0:T(8,128)(2,1)} %param.11), kind=kOutput, calls=%fused_computation | convolution fusion | flops 2422210560 | bytes 23199744 | tf_op jit(solution)/shard_map/slch,ldh->slcd/dot_general | solution.py:104
  383.4 11.2 %reshape.108 = bf16[64,24,2,1024]{3,2,0,1:T(2,128)(2,1)} reshape(bf16[64,2,12,2048]{3,0,2,1:T(8,128)(2,1)} %add_bitcast_fusion) | data formatting | bytes 12582912 | tf_op jit(solution)/shard_map/reshape | solution.py:68
  394.6 12.2 %copy.93 = bf16[64,2,24,1024]{3,2,1,0:T(8,128)(2,1)} copy(bf16[64,2,24,1024]{3,1,0,2:T(2,128)(2,1)} %bitcast.158) | data formatting | bytes 12582912 | tf_op jit(solution)/shard_map/transpose | solution.py:69
  406.7 7.5 %all-to-all-start.3 = ((bf16[128,24,1024]{2,1,0:T(8,128)(2,1)}), bf16[128,24,1024]{2,1,0:T(8,128)(2,1)}, u32[]{:S(2)}, u32[]{:S(2)}) async-start(bf16[128,24,1024]{2,1,0:T(8,128)(2,1)} %bitcast.153), calls=%async_computation.3 | async-start | bytes 12582912 | tf_op jit(solution)/shard_map/all_to_all | solution.py:70
  416.1 7.5 %bitcast_convert_fusion = bf16[2,384,2048]{2,1,0:T(8,128)(2,1)} fusion(bf16[64,2,12,384]{3,0,2,1:T(8,128)(2,1)S(1)} %copy-done.15, bf16[64,2,12,2048]{3,0,2,1:T(8,128)(2,1)} %reshape.107), kind=kOutput, calls=%fused_computation.4 | convolution fusion | flops 2417491968 | bytes 10616832 | tf_op jit(solution)/shard_map/slch,slcd->lhd/dot_general | solution.py:88
  423.6 4.9 bitcast_convert_fusion.1
  428.5 5.1 bitcast_convert_fusion.2
  433.6 9.8 %fusion.26 = f32[128,1024]{1,0:T(8,128)S(1)} fusion(bf16[64,2,24,1024]{3,2,1,0:T(8,128)(2,1)} %bitcast.19, bf16[128,64,24]{0,1,2:T(8,128)(2,1)S(1)} %copy.83), kind=kOutput, calls=%fused_computation.44 | convolution fusion | flops 805306368 | bytes 7208960 | tf_op jit(solution)/shard_map/tocr,ocrd->td/dot_general | solution.py:74
  443.4 10.8 %fusion.38 = bf16[128,1024]{1,0:T(8,128)(2,1)} fusion(f32[128,1024]{1,0:T(8,128)S(1)} %fusion.26, bf16[64,2,24,1024]{3,2,1,0:T(8,128)(2,1)} %bitcast.19, bf16[128,64,24]{0,1,2:T(8,128)(2,1)S(1)} %copy.87), kind=kOutput, calls=%fused_computation.48 | convolution fusion | flops 805568512 | bytes 7471104 | tf_op jit(solution)/shard_map/tocr,ocrd->td/dot_general | solution.py:74
  454.9 43.8 %all-to-all-done.3 = bf16[128,24,1024]{2,1,0:T(8,128)(2,1)} async-done(((bf16[128,24,1024]{2,1,0:T(8,128)(2,1)}), bf16[128,24,1024]{2,1,0:T(8,128)(2,1)}, u32[]{:S(2)}, u32[]{:S(2)}) %all-to-all-start.3) | async-done | bytes 6291488 | tf_op jit(solution)/shard_map/all_to_all | solution.py:70
  498.7 10.7 %fusion.41 = bf16[128,1024]{1,0:T(8,128)(2,1)} fusion(bf16[64,2,24,1024]{3,2,1,0:T(8,128)(2,1)} %bitcast.38, bf16[128,64,24]{0,1,2:T(8,128)(2,1)S(1)} %copy.90), kind=kOutput, calls=%fused_computation.49 | convolution fusion | flops 805437440 | bytes 6946816 | tf_op jit(solution)/shard_map/tocr,ocrd->td/dot_general | solution.py:74
  (71 shorter events, 9.0 us)
Async XLA Ops:
  0.6 238.9 %copy-start = (bf16[2,384,2048]{2,1,0:T(8,128)(2,1)S(1)}, bf16[2,384,2048]{2,1,0:T(8,128)(2,1)}, u32[]{:S(2)}) copy-start(bf16[2,384,2048]{2,1,0:T(8,128)(2,1)} %param.12) | copy-start | bytes 9437188
  0.6 4.0 copy-start.12
  2.1 0.8 copy-start.5
  13.5 10.5 %copy-start.13 = (f32[128,8]{0,1:T(8,128)S(1)}, f32[128,8]{0,1:T(8,128)}, u32[]{:S(2)}) copy-start(f32[128,8]{0,1:T(8,128)} %param.9) | copy-start | bytes 12292
  13.5 90.0 %all-to-all-start = ((bf16[64,24,2048]{2,1,0:T(8,128)(2,1)}), bf16[64,24,2048]{2,1,0:T(8,128)(2,1)}, u32[]{:S(2)}, u32[]{:S(2)}) async-start(bf16[64,24,2048]{2,1,0:T(8,128)(2,1)} %bitcast.152), calls=%async_computation | async-start | bytes 12582912 | tf_op jit(solution)/shard_map/all_to_all | solution.py:41
  227.2 6.6 %copy-start.2 = (bf16[2,2048,384]{2,1,0:T(8,128)(2,1)S(1)}, bf16[2,2048,384]{2,1,0:T(8,128)(2,1)}, u32[]{:S(2)}) copy-start(bf16[2,2048,384]{2,1,0:T(8,128)(2,1)} %param.10) | copy-start | bytes 9437188
  227.2 12.3 %slice-start.2 = ((s8[6291456]{0:T(1024)(128)(4,1)}), s8[4194304]{0:T(1024)(128)(4,1)S(1)}, s32[]{:S(2)}) async-start(s8[6291456]{0:T(1024)(128)(4,1)} %bitcast.166), calls=%async_computation.6 | async-start | bytes 8388608
  233.8 5.7 %slice-start.3 = ((s8[6291456]{0:T(1024)(128)(4,1)}), s8[2097152]{0:T(1024)(128)(4,1)S(1)}, s32[]{:S(2)}) async-start(s8[6291456]{0:T(1024)(128)(4,1)} %bitcast.166), calls=%async_computation.7 | async-start | bytes 4194304
  245.0 1.0 copy-start.14
  274.8 8.4 %copy-start.3 = (bf16[2,2048,384]{2,1,0:T(8,128)(2,1)S(1)}, bf16[2,2048,384]{2,1,0:T(8,128)(2,1)}, u32[]{:S(2)}) copy-start(bf16[2,2048,384]{2,1,0:T(8,128)(2,1)} %param.10) | copy-start | bytes 9437188
  274.8 92.8 %all-to-all-start.2 = ((bf16[128,24,1024]{2,1,0:T(8,128)(2,1)}), bf16[128,24,1024]{2,1,0:T(8,128)(2,1)}, u32[]{:S(2)}, u32[]{:S(2)}) async-start(bf16[128,24,1024]{2,1,0:T(8,128)(2,1)} %bitcast.154), calls=%async_computation.2 | async-start | bytes 12582912 | tf_op jit(solution)/shard_map/all_to_all | solution.py:70
  367.6 6.1 %copy-start.7 = (bf16[64,2,12,384]{3,0,2,1:T(8,128)(2,1)S(1)}, bf16[64,2,12,384]{3,0,2,1:T(8,128)(2,1)}, u32[]{:S(2)}) copy-start(bf16[64,2,12,384]{3,0,2,1:T(8,128)(2,1)} %get-tuple-element.30) | copy-start | bytes 3538948
  373.6 9.8 %copy-start.8 = (f32[128,8]{1,0:T(8,128)}, f32[128,8]{1,0:T(8,128)S(1)}, u32[]{:S(2)}) copy-start(f32[128,8]{1,0:T(8,128)S(1)} %select_reduce_fusion.2) | copy-start | bytes 12292
  373.6 9.8 %collective-permute-start = (f32[128,8]{1,0:T(8,128)S(1)}, f32[128,8]{1,0:T(8,128)S(1)}, u32[]{:S(2)}, u32[]{:S(2)}) collective-permute-start(f32[128,8]{1,0:T(8,128)S(1)} %select_reduce_fusion.2), channel_id=1, source_target_pairs={{0,1},{1,0},{2,3},{3,2},{4,5},{5,4},{6,7},{7,6},{8,9},{9,8},{10,11... | collective-permute-start | bytes 12296 | tf_op jit(solution)/shard_map/ppermute | solution.py:105
  383.4 11.2 %copy-start.10 = (f32[128,8]{1,0:T(8,128)}, f32[128,8]{1,0:T(8,128)S(1)}, u32[]{:S(2)}) copy-start(f32[128,8]{1,0:T(8,128)S(1)} %collective-permute-done) | copy-start | bytes 12292
  406.7 7.9 %copy-start.4 = (f32[128,1536]{1,0:T(8,128)S(1)}, f32[128,1536]{1,0:T(8,128)}, u32[]{:S(2)}) copy-start(f32[128,1536]{1,0:T(8,128)} %get-tuple-element.26) | copy-start | bytes 2359300
  406.7 92.0 %all-to-all-start.3 = ((bf16[128,24,1024]{2,1,0:T(8,128)(2,1)}), bf16[128,24,1024]{2,1,0:T(8,128)(2,1)}, u32[]{:S(2)}, u32[]{:S(2)}) async-start(bf16[128,24,1024]{2,1,0:T(8,128)(2,1)} %bitcast.153), calls=%async_computation.3 | async-start | bytes 12582912 | tf_op jit(solution)/shard_map/all_to_all | solution.py:70
  414.8 1.3 copy-start.15
  414.9 8.7 %slice-start = ((s8[6291456]{0:T(1024)(128)(4,1)}), s8[4194304]{0:T(1024)(128)(4,1)S(1)}, s32[]{:S(2)}) async-start(s8[6291456]{0:T(1024)(128)(4,1)} %bitcast.162), calls=%async_computation.4 | async-start | bytes 8388608
  416.1 7.5 %slice-start.1 = ((s8[6291456]{0:T(1024)(128)(4,1)}), s8[2097152]{0:T(1024)(128)(4,1)S(1)}, s32[]{:S(2)}) async-start(s8[6291456]{0:T(1024)(128)(4,1)} %bitcast.162), calls=%async_computation.5 | async-start | bytes 4194304
  423.6 4.9 copy-start.6
  443.4 10.8 %copy-start.9 = (f32[128,8]{1,0:T(8,128)S(1)}, f32[128,8]{1,0:T(8,128)}, u32[]{:S(2)}) copy-start(f32[128,8]{1,0:T(8,128)} %copy-done.8) | copy-start | bytes 12292
  443.4 10.8 %copy-start.11 = (f32[128,8]{1,0:T(8,128)S(1)}, f32[128,8]{1,0:T(8,128)}, u32[]{:S(2)}) copy-start(f32[128,8]{1,0:T(8,128)} %copy-done.10) | copy-start | bytes 12292
  498.7 10.7 %copy-start.1 = (bf16[2,384,2048]{2,1,0:T(8,128)(2,1)S(1)}, bf16[2,384,2048]{2,1,0:T(8,128)(2,1)}, u32[]{:S(2)}) copy-start(bf16[2,384,2048]{2,1,0:T(8,128)(2,1)} %param.12) | copy-start | bytes 9437188

commit v4 on v3

--- a/solution.py
+++ b/solution.py
@@ -1,7 +1,153 @@
 import jax
 import jax.numpy as jnp
 from jax import lax
+from jax.experimental import pallas as pl
+from jax.experimental.pallas import tpu as pltpu
 from jax.sharding import PartitionSpec as P
+
+MESH_ID = pl.DeviceIdType.MESH
+
+
+def _where(me_dp, me_col):
+    return me_dp * 2 + me_col
+
+
+def _dispatch_kernel(tok_ref, cot_ref, rows_ref, dout_ref, send_sems, recv_sems):
+    owners, rows, half = tok_ref.shape
+    me_dp, me_col = lax.axis_index("dp"), lax.axis_index("col")
+    count = owners * 2
+    me = _where(me_dp, me_col)
+    here = pl.ds(pl.multiple_of(me_col * half, half), half)
+    srcs, dsts = (tok_ref, cot_ref), (rows_ref, dout_ref)
+
+    def remote(kind, target):
+        t_dp, t_col = target // 2, target % 2
+        return pltpu.make_async_remote_copy(
+            src_ref=srcs[kind].at[t_dp],
+            dst_ref=dsts[kind].at[me_dp, :, here],
+            send_sem=send_sems.at[kind, target],
+            recv_sem=recv_sems.at[kind, me],
+            device_id=(t_dp, t_col),
+            device_id_type=MESH_ID,
+        )
+
+    def incoming(kind, source):
+        s_dp, s_col = source // 2, source % 2
+        there = pl.ds(pl.multiple_of(s_col * half, half), half)
+        return pltpu.make_async_remote_copy(
+            src_ref=srcs[kind].at[0],
+            dst_ref=dsts[kind].at[s_dp, :, there],
+            send_sem=send_sems.at[kind, source],
+            recv_sem=recv_sems.at[kind, source],
+            device_id=(s_dp, s_col),
+            device_id_type=MESH_ID,
+        )
+
+    for kind in range(2):
+        pltpu.make_async_copy(
+            srcs[kind].at[me_dp], dsts[kind].at[me_dp, :, here], recv_sems.at[kind, me]
+        ).start()
+
+    def start(i, carry):
+        target = lax.rem(me + i, count)
+        for kind in range(2):
+            remote(kind, target).start()
+        return carry
+
+    lax.fori_loop(1, count, start, 0)
+
+    def finish(i, carry):
+        other = lax.rem(me + i, count)
+        for kind in range(2):
+            remote(kind, other).wait_send()
+            incoming(kind, other).wait_recv()
+        return carry
+
+    lax.fori_loop(1, count, finish, 0)
+    for kind in range(2):
+        pltpu.make_async_copy(
+            srcs[kind].at[me_dp], dsts[kind].at[me_dp, :, here], recv_sems.at[kind, me]
+        ).wait()
+
+
+def _return_kernel(part_ref, recv_ref, send_sems, recv_sems):
+    sources, rows, width = part_ref.shape
+    half = width // 2
+    me_dp, me_col = lax.axis_index("dp"), lax.axis_index("col")
+    count = sources * 2
+    me = _where(me_dp, me_col)
+
+    def window(target):
+        cols = pl.ds(pl.multiple_of((target % 2) * half, half), half)
+        return part_ref.at[target // 2, :, cols]
+
+    def remote(target):
+        return pltpu.make_async_remote_copy(
+            src_ref=window(target),
+            dst_ref=recv_ref.at[me],
+            send_sem=send_sems.at[target],
+            recv_sem=recv_sems.at[me],
+            device_id=(target // 2, target % 2),
+            device_id_type=MESH_ID,
+        )
+
+    def incoming(source):
+        return pltpu.make_async_remote_copy(
+            src_ref=window(source),
+            dst_ref=recv_ref.at[source],
+            send_sem=send_sems.at[source],
+            recv_sem=recv_sems.at[source],
+            device_id=(source // 2, source % 2),
+            device_id_type=MESH_ID,
+        )
+
+    pltpu.make_async_copy(window(me), recv_ref.at[me], recv_sems.at[me]).start()
+
+    def start(i, carry):
+        remote(lax.rem(me + i, count)).start()
+        return carry
+
+    lax.fori_loop(1, count, start, 0)
+
+    def finish(i, carry):
+        other = lax.rem(me + i, count)
+        remote(other).wait_send()
+        incoming(other).wait_recv()
+        return carry
+
+    lax.fori_loop(1, count, finish, 0)
+    pltpu.make_async_copy(window(me), recv_ref.at[me], recv_sems.at[me]).wait()
+
+
+def dispatch(tok_half, cot_half):
+    owners, rows, half = tok_half.shape
+    full = jax.ShapeDtypeStruct((owners, rows, 2 * half), tok_half.dtype)
+    return pl.pallas_call(
+        _dispatch_kernel,
+        out_shape=(full, full),
+        in_specs=[pl.BlockSpec(memory_space=pl.ANY)] * 2,
+        out_specs=(pl.BlockSpec(memory_space=pl.ANY),) * 2,
+        scratch_shapes=[
+            pltpu.SemaphoreType.DMA((2, owners * 2)),
+            pltpu.SemaphoreType.DMA((2, owners * 2)),
+        ],
+        compiler_params=pltpu.CompilerParams(has_side_effects=True),
+    )(tok_half, cot_half)
+
+
+def send_home(part):
+    sources, rows, width = part.shape
+    return pl.pallas_call(
+        _return_kernel,
+        out_shape=jax.ShapeDtypeStruct((sources * 2, rows, width // 2), part.dtype),
+        in_specs=[pl.BlockSpec(memory_space=pl.ANY)],
+        out_specs=pl.BlockSpec(memory_space=pl.ANY),
+        scratch_shapes=[
+            pltpu.SemaphoreType.DMA((sources * 2,)),
+            pltpu.SemaphoreType.DMA((sources * 2,)),
+        ],
+        compiler_params=pltpu.CompilerParams(has_side_effects=True),
+    )(part)
 
 
 def body(tokens, routes, probs, w_gate, w_up, w_down, cotangent):
@@ -35,28 +181,19 @@
 
     both = ("dp", "col")
 
+    my_cols = lax.axis_index("col") * half_width
+    tok_half = lax.dynamic_slice_in_dim(tokens, my_cols, half_width, axis=1)
     send_tok = jnp.einsum(
-        "ts,td->sd", picker, tokens, preferred_element_type=jnp.float32
-    ).astype(jnp.bfloat16)
-    arrived_rows = lax.all_to_all(
-        send_tok.reshape(owners, rows_per_owner, width), "dp", 0, 0, tiled=True
+        "ts,td->sd", picker, tok_half, preferred_element_type=jnp.float32
+    ).astype(jnp.bfloat16)
+    cot_rows = jnp.einsum("ts,td->sd", picker, cotangent, preferred_element_type=jnp.float32)
+    send_cot = (prob_of_slot[:, None] * cot_rows).astype(jnp.bfloat16)
+    arrived_rows, arrived_cot = dispatch(
+        send_tok.reshape(owners, rows_per_owner, half_width),
+        send_cot.reshape(owners, rows_per_owner, half_width),
     )
     row_block = arrived_rows.reshape(owners, local_experts, slot_cap, width)
-
-    cot_rows = jnp.einsum("ts,td->sd", picker, cotangent, preferred_element_type=jnp.float32)
-    send_cot = (prob_of_slot[:, None] * cot_rows).astype(jnp.bfloat16)
-    send_cot = jnp.broadcast_to(
-        send_cot.reshape(owners, 1, rows_per_owner, half_width),
-        (owners, cols, rows_per_owner, half_width),
-    ).reshape(owners * cols, rows_per_owner, half_width)
-    arrived_cot = lax.all_to_all(send_cot, both, 0, 0, tiled=True)
-    arrived_rows, arrived_cot = lax.optimization_barrier((arrived_rows, arrived_cot))
-    row_block = arrived_rows.reshape(owners, local_experts, slot_cap, width)
-    d_out = (
-        arrived_cot.reshape(owners, cols, rows_per_owner, half_width)
-        .transpose(0, 2, 1, 3)
-        .reshape(owners, local_experts, slot_cap, width)
-    )
+    d_out = arrived_cot.reshape(owners, local_experts, slot_cap, width)
 
     def per_half(table):
         return jnp.broadcast_to(
@@ -65,10 +202,8 @@
         )
 
     def send_back(partial_value):
-        part = partial_value.astype(jnp.bfloat16).reshape(owners, rows_per_owner, cols, half_width)
-        part = part.transpose(0, 2, 1, 3).reshape(owners * cols, rows_per_owner, half_width)
-        got = lax.all_to_all(part, both, 0, 0, tiled=True)
-        return got.reshape(owners, cols, rows_per_owner, half_width)
+        part = partial_value.astype(jnp.bfloat16).reshape(owners, rows_per_owner, width)
+        return send_home(part).reshape(owners, cols, rows_per_owner, half_width)
 
     def combine(table, got):
         return jnp.einsum("tocr,ocrd->td", per_half(table), got, preferred_element_type=jnp.float32)
@@ -103,7 +238,6 @@
         "slch,ldh->slcd", d_gate, w_gate, preferred_element_type=jnp.float32
     ) + jnp.einsum("slch,ldh->slcd", d_up, w_up, preferred_element_type=jnp.float32)
     prob_other = lax.ppermute(prob_part, "col", perm=[(0, 1), (1, 0)])
-    prob_other, d_partial = lax.optimization_barrier((prob_other, d_partial))
     got_grad = send_back(d_partial)
     grad_tokens = combine(picker, got_grad).astype(jnp.bfloat16)
     grad_probs = prob_part + prob_other

time: 518 us -> 624 us (1.20)
  the two profiles are of different devices: /device:TPU:98 before, /device:TPU:25 now
where the time goes in v4:
time: 624 us; the launch traced here: 618 us
  Pallas kernels  477 us (76%)
  matrix products  98.8 us (16%)
  local copies, waits for them, and re-layouts  30.8 us (5%)
  other arithmetic  10.7 us (2%)
    pallas_call x2, Pallas kernels, send_home(): pl.pallas_call(_return_kernel, out_shape=jax.ShapeDtypeStruct((sources *...  248 us
    pallas_call x1, Pallas kernels, dispatch(): pl.pallas_call(_dispatch_kernel, out_shape=(full, full), in_specs=[pl.Blo...  229 us
    dot_general x3, matrix products, combine(): jnp.einsum('tocr,ocrd->td', per_half(table), got, preferred_element_type=...  26.5 us
    reshape x2, local copies, waits for them, and re-layouts, send_back(): partial_value.astype(jnp.bfloat16).reshape(owners, rows_per_owner, width)  14.9 us
  transfers between devices with their start and end apart: 1, of which 0 were waited for; matrix products, arithmetic and copies ran while one was open for 12% of the time, Pallas kernels for 19%

profile of v4, /device:TPU:25, one launch (start us, length us, event | category | flops | bytes accessed | tf_op | source)
XLA Modules:
  0.0 618.5 jit_solution(6866477552825018838)
XLA Ops:
  0.7 0.9 copy.65
  1.9 0.8 copy.71
  2.9 0.8 copy-done.8
  3.7 1.1 broadcast_add_fusion
  5.5 3.2 fusion.2
  8.7 3.3 select_reduce_fusion.1
  12.0 3.7 convolution_convert_fusion.1
  15.7 2.7 multiply_convert_fusion
  18.4 228.9 %shard_map.118 = (bf16[64,24,2048]{2,1,0:T(8,128)(2,1)}, bf16[64,24,2048]{2,1,0:T(8,128)(2,1)}) custom-call(bf16[64,24,1024]{2,1,0:T(8,128)(2,1)} %bitcast.140, bf16[64,24,1024]{2,1,0:T(8,128)(2,1)} %bitcast.139), custom_call_target="tpu_custom_call" | custom-call | tf_op jit(solution)/shard_map/pallas_call | solution.py:125
  247.3 6.2 %copy.74 = bf16[64,24,2048]{2,0,1:T(8,128)(2,1)S(1)} copy(bf16[64,24,2048]{2,1,0:T(8,128)(2,1)} %get-tuple-element.8) | data formatting | bytes 12582912 | tf_op jit(solution)/shard_map/pallas_call | solution.py:125
  253.6 9.0 %fusion.8 = f32[2,64,12,384]{3,1,2,0:T(8,128)} fusion(bf16[64,2,12,2048]{3,0,2,1:T(8,128)(2,1)S(1)} %bitcast.141, bf16[2,2048,384]{2,1,0:T(8,128)(2,1)} %param.11), kind=kOutput, calls=%fused_computation.19 | convolution fusion | flops 2415919104 | bytes 11796480 | tf_op jit(solution)/shard_map/slcd,ldh->slch/dot_general | solution.py:212
  262.6 4.8 fusion.12
  267.5 3.9 copy.81
  271.4 7.6 %fusion.20 = (bf16[64,2,12,384]{3,0,2,1:T(8,128)(2,1)}, bf16[64,2,12,384]{3,0,2,1:T(8,128)(2,1)}, bf16[64,2,12,384]{3,0,2,1:T(8,128)(2,1)S(1)}) fusion(f32[2,64,12,384]{3,1,2,0:T(8,128)} %fusion.12, f32[2,64,12,384]{3,1,2,0:T(8,128)S(1)} %copy-done.17, bf16[64,2,12,2048]{3,0,2,1:T(8,128)(2,1)S(1)} %bitcast.152, bf16[2,384,2048]{2,1,0:T(8,128)(2,1)S(1)} %copy-done), kind=kOutput, calls=%fused_computation.33 | convolution fusion | flops 2424766464 | bytes 17694720 | tf_op jit(solution)/shard_map/slcd,lhd->slch/dot_general | solution.py:226
  279.0 3.6 convolution_convert_fusion
  282.7 6.1 copy.75.part_ref
  288.7 129.5 %shard_map.119 = bf16[128,24,1024]{2,1,0:T(8,128)(2,1)} custom-call(bf16[64,24,2048]{2,1,0:T(8,128)(2,1)} %copy.75.part_ref), custom_call_target="tpu_custom_call" | custom-call | tf_op jit(solution)/shard_map/pallas_call | solution.py:140
  418.2 4.7 convolution_reduce_fusion
  423.3 1.6 select_reduce_fusion.2
  424.9 7.3 %bitcast_convert_fusion = bf16[2,384,2048]{2,1,0:T(8,128)(2,1)} fusion(bf16[64,2,12,384]{3,0,2,1:T(8,128)(2,1)S(1)} %copy-done.16, bf16[64,2,12,2048]{3,0,2,1:T(8,128)(2,1)} %bitcast.153), kind=kOutput, calls=%fused_computation.3 | convolution fusion | flops 2417491968 | bytes 10616832 | tf_op jit(solution)/shard_map/slch,slcd->lhd/dot_general | solution.py:223
  432.2 4.9 bitcast_convert_fusion.2
  437.1 6.5 %fusion.10 = f32[2,64,12,2048]{3,1,2,0:T(8,128)} fusion(bf16[64,2,12,384]{3,0,2,1:T(8,128)(2,1)S(1)} %copy-done.9, bf16[2,2048,384]{2,1,0:T(8,128)(2,1)S(1)} %copy-done.6), kind=kOutput, calls=%fused_computation.21 | convolution fusion | flops 2415919104 | bytes 16908288 | tf_op jit(solution)/shard_map/slch,ldh->slcd/dot_general | solution.py:237
  444.3 0.9 copy.77
  445.3 8.8 %bitcast_convert_fusion.1 = bf16[2,2048,384]{2,1,0:T(8,128)(2,1)} fusion(bf16[64,2,12,2048]{3,0,2,1:T(8,128)(2,1)} %bitcast.143, bf16[64,2,12,384]{3,0,2,1:T(8,128)(2,1)} %get-tuple-element.26), kind=kOutput, calls=%fused_computation.4 | convolution fusion | flops 2417491968 | bytes 10616832 | tf_op jit(solution)/shard_map/slcd,slch->ldh/dot_general | solution.py:234
  454.1 7.8 %fusion.26 = f32[128,1024]{1,0:T(8,128)} fusion(bf16[64,2,24,1024]{3,2,1,0:T(8,128)(2,1)S(1)} %bitcast.151, bf16[128,64,24]{0,1,2:T(8,128)(2,1)S(1)} %copy.73), kind=kOutput, calls=%fused_computation.44 | convolution fusion | flops 805306368 | bytes 7208960 | tf_op jit(solution)/shard_map/tocr,ocrd->td/dot_general | solution.py:209
  462.0 8.6 %add_convert_fusion = bf16[2,64,12,2048]{3,1,2,0:T(8,128)(2,1)} fusion(f32[2,64,12,2048]{3,1,2,0:T(8,128)S(1)} %bitcast.137, bf16[64,2,12,384]{3,0,2,1:T(8,128)(2,1)} %get-tuple-element.26, bf16[2,2048,384]{2,1,0:T(8,128)(2,1)} %param.11), kind=kOutput, calls=%fused_computation | convolution fusion | flops 2422210560 | bytes 23199744 | tf_op jit(solution)/shard_map/slch,ldh->slcd/dot_general | solution.py:239
  470.6 8.9 %copy.82.part_ref = bf16[64,24,2048]{2,1,0:T(8,128)(2,1)} copy(bf16[64,24,2048]{2,0,1:T(8,128)(2,1)} %bitcast.138) | data formatting | bytes 12582912 | tf_op jit(solution)/shard_map/reshape | solution.py:205
  479.4 118.3 %shard_map.120 = bf16[128,24,1024]{2,1,0:T(8,128)(2,1)} custom-call(bf16[64,24,2048]{2,1,0:T(8,128)(2,1)} %copy.82.part_ref), custom_call_target="tpu_custom_call" | custom-call | tf_op jit(solution)/shard_map/pallas_call | solution.py:140
  597.8 10.7 %fusion.38 = bf16[128,1024]{1,0:T(8,128)(2,1)} fusion(f32[128,1024]{1,0:T(8,128)S(1)} %copy-done.14, bf16[64,2,24,1024]{3,2,1,0:T(8,128)(2,1)} %bitcast.148, bf16[128,64,24]{0,1,2:T(8,128)(2,1)S(1)} %copy-done.10), kind=kOutput, calls=%fused_computation.48 | convolution fusion | flops 805568512 | bytes 7471104 | tf_op jit(solution)/shard_map/tocr,ocrd->td/dot_general | solution.py:209
  608.5 8.0 %fusion.41 = bf16[128,1024]{1,0:T(8,128)(2,1)} fusion(bf16[64,2,24,1024]{3,2,1,0:T(8,128)(2,1)S(1)} %bitcast.156, bf16[128,64,24]{0,1,2:T(8,128)(2,1)S(1)} %copy.80), kind=kOutput, calls=%fused_computation.49 | convolution fusion | flops 805437440 | bytes 6946816 | tf_op jit(solution)/shard_map/tocr,ocrd->td/dot_general | solution.py:209
  616.5 0.9 add.30
  617.4 0.7 copy.85
  (79 shorter events, 2.4 us)
Async XLA Ops:
  0.6 270.8 %copy-start = (bf16[2,384,2048]{2,1,0:T(8,128)(2,1)S(1)}, bf16[2,384,2048]{2,1,0:T(8,128)(2,1)}, u32[]{:S(2)}) copy-start(bf16[2,384,2048]{2,1,0:T(8,128)(2,1)} %param.12) | copy-start | bytes 9437188
  0.6 4.8 copy-start.13
  2.9 0.8 copy-start.8
  12.0 3.7 copy-start.11
  253.6 9.1 %copy-start.2 = (bf16[64,24,2048]{2,0,1:T(8,128)(2,1)}, bf16[64,24,2048]{2,0,1:T(8,128)(2,1)S(1)}, u32[]{:S(2)}) copy-start(bf16[64,24,2048]{2,0,1:T(8,128)(2,1)S(1)} %copy.74) | copy-start | bytes 18874372
  253.6 9.0 %copy-start.5 = (bf16[2,2048,384]{2,1,0:T(8,128)(2,1)S(1)}, bf16[2,2048,384]{2,1,0:T(8,128)(2,1)}, u32[]{:S(2)}) copy-start(bf16[2,2048,384]{2,1,0:T(8,128)(2,1)} %param.10) | copy-start | bytes 9437188
  253.6 13.9 %slice-start.7 = ((s8[6291456]{0:T(1024)(128)(4,1)}), s8[4194304]{0:T(1024)(128)(4,1)S(1)}, s32[]{:S(2)}) async-start(s8[6291456]{0:T(1024)(128)(4,1)} %bitcast.154), calls=%async_computation.7 | async-start | bytes 8388608
  262.6 4.8 slice-start.8
  267.5 3.9 copy-start.17
  271.4 7.6 %copy-start.3 = (bf16[64,24,2048]{2,0,1:T(8,128)(2,1)}, bf16[64,24,2048]{2,0,1:T(8,128)(2,1)S(1)}, u32[]{:S(2)}) copy-start(bf16[64,24,2048]{2,0,1:T(8,128)(2,1)S(1)} %copy.81) | copy-start | bytes 18874372
  279.0 3.6 copy-start.15
  288.7 129.5 %copy-start.12 = (bf16[128,1024]{1,0:T(8,128)(2,1)S(1)}, bf16[128,1024]{1,0:T(8,128)(2,1)}, u32[]{:S(2)}) copy-start(bf16[128,1024]{1,0:T(8,128)(2,1)} %param.13) | copy-start | bytes 786436
  418.2 6.6 %copy-start.16 = (bf16[64,2,12,384]{3,0,2,1:T(8,128)(2,1)S(1)}, bf16[64,2,12,384]{3,0,2,1:T(8,128)(2,1)}, u32[]{:S(2)}) copy-start(bf16[64,2,12,384]{3,0,2,1:T(8,128)(2,1)} %copy-done.15) | copy-start | bytes 3538948
  423.3 8.9 %slice-start.3 = ((s8[6291456]{0:T(1024)(128)(4,1)}), s8[4194304]{0:T(1024)(128)(4,1)S(1)}, s32[]{:S(2)}) async-start(s8[6291456]{0:T(1024)(128)(4,1)} %bitcast.144), calls=%async_computation.3 | async-start | bytes 8388608
  424.8 191.7 %collective-permute-start = (f32[128,8]{1,0:T(8,128)}, f32[128,8]{1,0:T(8,128)}, u32[]{:S(2)}, u32[]{:S(2)}) collective-permute-start(f32[128,8]{1,0:T(8,128)} %select_reduce_fusion.2), channel_id=1, source_target_pairs={{0,1},{1,0},{2,3},{3,2},{4,5},{5,4},{6,7},{7,6},{8,9},{9,8},{10,11... | collective-permute-start | bytes 12296 | tf_op jit(solution)/shard_map/ppermute | solution.py:240
  424.9 7.3 %slice-start.4 = ((s8[6291456]{0:T(1024)(128)(4,1)}), s8[2097152]{0:T(1024)(128)(4,1)S(1)}, s32[]{:S(2)}) async-start(s8[6291456]{0:T(1024)(128)(4,1)} %bitcast.144), calls=%async_computation.4 | async-start | bytes 4194304
  424.9 7.3 %copy-start.9 = (bf16[64,2,12,384]{3,0,2,1:T(8,128)(2,1)S(1)}, bf16[64,2,12,384]{3,0,2,1:T(8,128)(2,1)}, u32[]{:S(2)}) copy-start(bf16[64,2,12,384]{3,0,2,1:T(8,128)(2,1)} %get-tuple-element.27) | copy-start | bytes 3538948
  432.2 4.9 copy-start.6
  437.1 6.8 %copy-start.7 = (f32[128,1536]{1,0:T(8,128)S(1)}, f32[128,1536]{1,0:T(8,128)}, u32[]{:S(2)}) copy-start(f32[128,1536]{1,0:T(8,128)} %get-tuple-element.22) | copy-start | bytes 2359300
  444.3 9.8 %slice-start.5 = ((s8[6291456]{0:T(1024)(128)(4,1)}), s8[4194304]{0:T(1024)(128)(4,1)S(1)}, s32[]{:S(2)}) async-start(s8[6291456]{0:T(1024)(128)(4,1)} %bitcast.149), calls=%async_computation.5 | async-start | bytes 8388608
  445.2 16.8 %slice-start = ((s8[12582912]{0:T(1024)(128)(4,1)}), s8[4194304]{0:T(1024)(128)(4,1)S(1)}, s32[]{:S(2)}) async-start(s8[12582912]{0:T(1024)(128)(4,1)} %bitcast.136), calls=%async_computation | async-start | bytes 8388608
  445.3 8.8 %slice-start.6 = ((s8[6291456]{0:T(1024)(128)(4,1)}), s8[2097152]{0:T(1024)(128)(4,1)S(1)}, s32[]{:S(2)}) async-start(s8[6291456]{0:T(1024)(128)(4,1)} %bitcast.149), calls=%async_computation.6 | async-start | bytes 4194304
  445.3 16.7 %slice-start.1 = ((s8[12582912]{0:T(1024)(128)(4,1)}), s8[4194304]{0:T(1024)(128)(4,1)S(1)}, s32[]{:S(2)}) async-start(s8[12582912]{0:T(1024)(128)(4,1)} %bitcast.136), calls=%async_computation.1 | async-start | bytes 8388608
  445.3 16.7 %slice-start.2 = ((s8[12582912]{0:T(1024)(128)(4,1)}), s8[4194304]{0:T(1024)(128)(4,1)S(1)}, s32[]{:S(2)}) async-start(s8[12582912]{0:T(1024)(128)(4,1)} %bitcast.136), calls=%async_computation.2 | async-start | bytes 8388608
  479.4 118.4 %copy-start.10 = (bf16[128,64,24]{0,1,2:T(8,128)(2,1)S(1)}, bf16[128,64,24]{0,1,2:T(8,128)(2,1)}, u32[]{:S(2)}) copy-start(bf16[128,64,24]{0,1,2:T(8,128)(2,1)} %copy.77) | copy-start | bytes 1179652
  479.4 118.4 %copy-start.14 = (f32[128,1024]{1,0:T(8,128)S(1)}, f32[128,1024]{1,0:T(8,128)}, u32[]{:S(2)}) copy-start(f32[128,1024]{1,0:T(8,128)} %fusion.26) | copy-start | bytes 1572868
  597.8 10.7 %copy-start.4 = (bf16[128,24,1024]{2,1,0:T(8,128)(2,1)S(1)}, bf16[128,24,1024]{2,1,0:T(8,128)(2,1)}, u32[]{:S(2)}) copy-start(bf16[128,24,1024]{2,1,0:T(8,128)(2,1)} %shard_map.120) | copy-start | bytes 18874372
  608.5 9.6 %copy-start.1 = (bf16[2,384,2048]{2,1,0:T(8,128)(2,1)S(1)}, bf16[2,384,2048]{2,1,0:T(8,128)(2,1)}, u32[]{:S(2)}) copy-start(bf16[2,384,2048]{2,1,0:T(8,128)(2,1)} %param.12) | copy-start | bytes 9437188

commit v5 on v1

--- a/solution.py
+++ b/solution.py
@@ -90,9 +90,11 @@
     d_partial = jnp.einsum(
         "slch,ldh->slcd", d_gate, w_gate, preferred_element_type=jnp.float32
     ) + jnp.einsum("slch,ldh->slcd", d_up, w_up, preferred_element_type=jnp.float32)
+    prob_other = lax.ppermute(prob_part, "col", perm=[(0, 1), (1, 0)])
+    prob_other, d_partial = lax.optimization_barrier((prob_other, d_partial))
     picked_grad = send_back(d_partial)
     grad_tokens = jnp.sum(picked_grad, axis=1).astype(jnp.bfloat16)
-    grad_probs = lax.psum(prob_part, "col")
+    grad_probs = prob_part + prob_other
     return (mixed, grad_tokens, grad_probs, grad_gate, grad_up, grad_down)
 
 

time: 495 us -> 548 us (1.11)
  the two profiles are of different devices: /device:TPU:82 before, /device:TPU:98 now
where the time goes in v5:
time: 548 us; the launch traced here: 540 us
  waiting for transfers between devices  265 us (48%)
  local copies, waits for them, and re-layouts  135 us (25%)
  matrix products  60.9 us (11%)
  starting transfers between devices  39.8 us (7%)
  other arithmetic  38.2 us (7%)
    all_to_all x2, waiting for transfers between devices, send_back(): got = lax.all_to_all(part, both, 0, 0, tiled=True)  135 us
    all_to_all x1, waiting for transfers between devices, body(): arrived_cot = lax.all_to_all(send_cot, both, 0, 0, tiled=True)  66.3 us
    all_to_all x1, waiting for transfers between devices, body(): lax.all_to_all(send_tok.reshape(owners, rows_per_owner, width), 'dp', 0,...  63.4 us
    transpose x2, local copies, waits for them, and re-layouts, send_back(): part.transpose(0, 2, 1, 3)  24.3 us
    reshape x2, local copies, waits for them, and re-layouts, send_back(): partial_value.astype(jnp.bfloat16)  22.2 us
    gather x2, local copies, waits for them, and re-layouts, send_back(): return summed[flat_index].reshape(tok_count, top_count, half_width)  18.5 us
    reduce_sum x2, other arithmetic, send_back(): summed = jnp.sum(got, axis=1).reshape(slots, half_width)  16 us
    all_to_all x1, starting transfers between devices, body(): arrived_cot = lax.all_to_all(send_cot, both, 0, 0, tiled=True)  14.9 us
  transfers between devices with their start and end apart: 5, of which 4 were waited for; matrix products, arithmetic and copies ran while one was open for 13% of the time, Pallas kernels for 0%

profile of v5, /device:TPU:98, one launch (start us, length us, event | category | flops | bytes accessed | tf_op | source)
XLA Modules:
  0.0 540.5 jit_solution(3544757203095877663)
XLA Ops:
  10.0 13.8 %gather_fusion = bf16[1536,2048]{1,0:T(8,128)(2,1)} fusion(bf16[128,2048]{1,0:T(8,128)(2,1)} %param.7, s32[2048]{0:T(1024)S(1)} %pad_clamp_fusion.1), kind=kCustom, calls=%fused_computation | custom fusion | bytes 12589056 | tf_op jit(solution)/shard_map/gather | solution.py:36
  23.8 5.9 %broadcast_select_fusion = bf16[64,24,2048]{2,1,0:T(8,128)(2,1)} fusion(bf16[64,24,2048]{2,1,0:T(8,128)(2,1)} %bitcast.147, pred[64,24]{1,0:T(8,128)(4,1)S(1)} %broadcast_in_dim.42), kind=kLoop, calls=%fused_computation.16 | loop fusion | flops 3145728 | bytes 12584448 | tf_op jit(solution)/shard_map/jit(_where)/select_n | solution.py:36
  29.7 10.5 %all-to-all-start = ((bf16[64,24,2048]{2,1,0:T(8,128)(2,1)}), bf16[64,24,2048]{2,1,0:T(8,128)(2,1)}, u32[]{:S(2)}, u32[]{:S(2)}) async-start(bf16[64,24,2048]{2,1,0:T(8,128)(2,1)} %broadcast_select_fusion), calls=%async_computation | async-start | bytes 12582912 | tf_op jit(solution)/shard_map/all_to_all | solution.py:37
  40.5 5.9 %gather_fusion.2 = f32[1536]{0:T(1024)S(1)} fusion(f32[1024]{0:T(1024)S(1)} %reshape.147, s32[2048]{0:T(1024)S(1)} %pad_clamp_fusion), kind=kCustom, calls=%fused_computation.2 | custom fusion | bytes 18432 | tf_op jit(solution)/shard_map/gather | solution.py:42
  46.4 5.8 %gather_fusion.3 = bf16[1536,1024]{1,0:T(8,128)(2,1)} fusion(bf16[128,1024]{1,0:T(8,128)(2,1)S(1)} %copy-done.2, s32[2048]{0:T(1024)S(1)} %pad_clamp_fusion.1), kind=kCustom, calls=%fused_computation.3 | custom fusion | bytes 6297600 | tf_op jit(solution)/shard_map/gather | solution.py:43
  56.3 63.4 %all-to-all-done = bf16[64,24,2048]{2,1,0:T(8,128)(2,1)} async-done(((bf16[64,24,2048]{2,1,0:T(8,128)(2,1)}), bf16[64,24,2048]{2,1,0:T(8,128)(2,1)}, u32[]{:S(2)}, u32[]{:S(2)}) %all-to-all-start) | async-done | bytes 6291488 | tf_op jit(solution)/shard_map/all_to_all | solution.py:37
  119.8 5.4 %broadcast_in_dim.49 = bf16[64,2,24,1024]{3,2,1,0:T(8,128)(2,1)} broadcast(bf16[64,24,1024]{2,1,0:T(8,128)(2,1)} %fusion), dimensions={0,2,3} | broadcast | bytes 9437184 | tf_op jit(solution)/shard_map/broadcast_in_dim | solution.py:46
  125.2 14.9 %all-to-all-start.2 = ((bf16[128,24,1024]{2,1,0:T(8,128)(2,1)}), bf16[128,24,1024]{2,1,0:T(8,128)(2,1)}, u32[]{:S(2)}, u32[]{:S(2)}) async-start(bf16[128,24,1024]{2,1,0:T(8,128)(2,1)} %bitcast.142), calls=%async_computation.2 | async-start | bytes 12582912 | tf_op jit(solution)/shard_map/all_to_all | solution.py:50
  140.1 6.4 %copy.32 = bf16[64,24,2048]{2,0,1:T(8,128)(2,1)S(1)} copy(bf16[64,24,2048]{2,1,0:T(8,128)(2,1)} %all-to-all-done) | data formatting | bytes 12582912 | tf_op jit(solution)/shard_map/all_to_all | solution.py:37
  146.5 4.8 fusion.4
  156.2 66.3 %all-to-all-done.2 = bf16[128,24,1024]{2,1,0:T(8,128)(2,1)} async-done(((bf16[128,24,1024]{2,1,0:T(8,128)(2,1)}), bf16[128,24,1024]{2,1,0:T(8,128)(2,1)}, u32[]{:S(2)}, u32[]{:S(2)}) %all-to-all-start.2) | async-done | bytes 6291488 | tf_op jit(solution)/shard_map/all_to_all | solution.py:50
  222.5 12.6 %copy.51 = bf16[64,2,24,1024]{3,1,0,2:T(2,128)(2,1)} copy(bf16[64,2,24,1024]{3,2,1,0:T(8,128)(2,1)} %bitcast.23) | data formatting | bytes 12582912 | tf_op jit(solution)/shard_map/reshape | solution.py:52
  235.1 11.5 %reshape.150 = bf16[64,2,12,2048]{3,0,2,1:T(8,128)(2,1)} reshape(bf16[64,24,2,1024]{3,2,0,1:T(2,128)(2,1)} %bitcast.144) | data formatting | bytes 12582912 | tf_op jit(solution)/shard_map/reshape | solution.py:54
  246.7 9.8 %fusion.16 = (bf16[64,2,12,384]{3,0,2,1:T(8,128)(2,1)}, bf16[64,2,12,384]{3,0,2,1:T(8,128)(2,1)}, bf16[64,2,12,384]{3,0,2,1:T(8,128)(2,1)S(1)}) fusion(f32[2,64,12,384]{3,1,2,0:T(8,128)} %fusion.8, f32[2,64,12,384]{3,1,2,0:T(8,128)} %fusion.4, bf16[64,2,12,2048]{3,0,2,1:T(8,128)(2,1)} %reshape.150, bf16[2,384,2048]{2,1,0:T(8,128)(2,1)S(1)} %copy-done), kind=kOutput, calls=%fused_computation.37 | convolution fusion | flops 2424766464 | bytes 17694720 | tf_op jit(solution)/shard_map/slcd,lhd->slch/dot_general | solution.py:79
  257.4 5.3 convert_bitcast_fusion
  262.7 11.1 %reshape.143 = bf16[64,24,2,1024]{3,2,0,1:T(2,128)(2,1)} reshape(bf16[64,2,12,2048]{3,0,2,1:T(8,128)(2,1)} %convert_bitcast_fusion) | data formatting | bytes 12582912 | tf_op jit(solution)/shard_map/reshape | solution.py:58
  273.9 12.2 %copy.33 = bf16[64,2,24,1024]{3,2,1,0:T(8,128)(2,1)} copy(bf16[64,2,24,1024]{3,1,0,2:T(2,128)(2,1)} %bitcast.145) | data formatting | bytes 12582912 | tf_op jit(solution)/shard_map/transpose | solution.py:59
  286.1 6.4 %all-to-all-start.1 = ((bf16[128,24,1024]{2,1,0:T(8,128)(2,1)}), bf16[128,24,1024]{2,1,0:T(8,128)(2,1)}, u32[]{:S(2)}, u32[]{:S(2)}) async-start(bf16[128,24,1024]{2,1,0:T(8,128)(2,1)} %bitcast.143), calls=%async_computation.1 | async-start | bytes 12582912 | tf_op jit(solution)/shard_map/all_to_all | solution.py:60
  293.4 7.6 %fusion.6 = f32[2,64,12,2048]{3,1,2,0:T(8,128)} fusion(bf16[64,2,12,384]{3,0,2,1:T(8,128)(2,1)} %get-tuple-element.21, bf16[2,2048,384]{2,1,0:T(8,128)(2,1)S(1)} %copy-done.5), kind=kOutput, calls=%fused_computation.25 | convolution fusion | flops 2415919104 | bytes 16908288 | tf_op jit(solution)/shard_map/slch,ldh->slcd/dot_general | solution.py:90
  300.9 74.0 %all-to-all-done.1 = bf16[128,24,1024]{2,1,0:T(8,128)(2,1)} async-done(((bf16[128,24,1024]{2,1,0:T(8,128)(2,1)}), bf16[128,24,1024]{2,1,0:T(8,128)(2,1)}, u32[]{:S(2)}, u32[]{:S(2)}) %all-to-all-start.1) | async-done | bytes 6291488 | tf_op jit(solution)/shard_map/all_to_all | solution.py:60
  374.9 8.0 %convert_reduce_fusion.1 = f32[64,24,1024]{2,1,0:T(8,128)} fusion(bf16[128,24,1024]{2,1,0:T(8,128)(2,1)} %all-to-all-done.1), kind=kLoop, calls=%fused_computation.7 | loop fusion | flops 4718592 | bytes 12582912 | tf_op jit(solution)/shard_map/reduce_sum | solution.py:62
  382.9 9.2 %gather_fusion.1 = f32[1024,1024]{1,0:T(8,128)} fusion(f32[1536,1024]{1,0:T(8,128)} %bitcast.140, s32[1024]{0:T(1024)S(1)} %broadcast_clamp_fusion), kind=kCustom, calls=%fused_computation.1 | custom fusion | bytes 8392704 | tf_op jit(solution)/shard_map/gather | solution.py:63
  396.9 8.4 %add_bitcast_fusion = bf16[64,2,12,2048]{3,0,2,1:T(8,128)(2,1)} fusion(f32[2,64,12,2048]{3,1,2,0:T(8,128)} %fusion.6, bf16[64,2,12,384]{3,0,2,1:T(8,128)(2,1)S(1)} %copy-done.10, bf16[2,2048,384]{2,1,0:T(8,128)(2,1)S(1)} %copy-done.7), kind=kOutput, calls=%fused_computation.8 | convolution fusion | flops 2422210560 | bytes 23199744 | tf_op jit(solution)/shard_map/slch,ldh->slcd/dot_general | solution.py:92
  405.3 11.1 %reshape.151 = bf16[64,24,2,1024]{3,2,0,1:T(2,128)(2,1)} reshape(bf16[64,2,12,2048]{3,0,2,1:T(8,128)(2,1)} %add_bitcast_fusion) | data formatting | bytes 12582912 | tf_op jit(solution)/shard_map/reshape | solution.py:58
  416.3 12.1 %copy.38 = bf16[64,2,24,1024]{3,2,1,0:T(8,128)(2,1)} copy(bf16[64,2,24,1024]{3,1,0,2:T(2,128)(2,1)} %bitcast.146) | data formatting | bytes 12582912 | tf_op jit(solution)/shard_map/transpose | solution.py:59
  428.5 7.9 %all-to-all-start.3 = ((bf16[128,24,1024]{2,1,0:T(8,128)(2,1)}), bf16[128,24,1024]{2,1,0:T(8,128)(2,1)}, u32[]{:S(2)}, u32[]{:S(2)}) async-start(bf16[128,24,1024]{2,1,0:T(8,128)(2,1)} %bitcast.141), calls=%async_computation.3 | async-start | bytes 12582912 | tf_op jit(solution)/shard_map/all_to_all | solution.py:60
  436.5 7.3 %bitcast_convert_fusion = bf16[2,384,2048]{2,1,0:T(8,128)(2,1)} fusion(bf16[64,2,12,384]{3,0,2,1:T(8,128)(2,1)S(1)} %copy-done.14, bf16[64,2,12,2048]{3,0,2,1:T(8,128)(2,1)} %reshape.150), kind=kOutput, calls=%fused_computation.11 | convolution fusion | flops 2417491968 | bytes 10616832 | tf_op jit(solution)/shard_map/slch,slcd->lhd/dot_general | solution.py:76
  443.7 8.1 %bitcast_convert_fusion.1 = bf16[2,2048,384]{2,1,0:T(8,128)(2,1)} fusion(bf16[64,2,12,2048]{3,0,2,1:T(8,128)(2,1)} %bitcast.151, bf16[64,2,12,384]{3,0,2,1:T(8,128)(2,1)S(1)} %copy-done.11), kind=kOutput, calls=%fused_computation.12 | convolution fusion | flops 2417491968 | bytes 10616832 | tf_op jit(solution)/shard_map/slcd,slch->ldh/dot_general | solution.py:87
  451.8 4.9 bitcast_convert_fusion.2
  457.4 61.4 %all-to-all-done.3 = bf16[128,24,1024]{2,1,0:T(8,128)(2,1)} async-done(((bf16[128,24,1024]{2,1,0:T(8,128)(2,1)}), bf16[128,24,1024]{2,1,0:T(8,128)(2,1)}, u32[]{:S(2)}, u32[]{:S(2)}) %all-to-all-start.3) | async-done | bytes 6291488 | tf_op jit(solution)/shard_map/all_to_all | solution.py:60
  518.8 8.0 %convert_reduce_fusion = f32[64,24,1024]{2,1,0:T(8,128)} fusion(bf16[128,24,1024]{2,1,0:T(8,128)(2,1)} %all-to-all-done.3), kind=kLoop, calls=%fused_computation.6 | loop fusion | flops 4718592 | bytes 12582912 | tf_op jit(solution)/shard_map/reduce_sum | solution.py:62
  526.8 9.3 %gather_fusion.4 = f32[1024,1024]{1,0:T(8,128)} fusion(f32[1536,1024]{1,0:T(8,128)} %bitcast.139, s32[1024]{0:T(1024)S(1)} %broadcast_clamp_fusion), kind=kCustom, calls=%fused_computation.4 | custom fusion | bytes 8392704 | tf_op jit(solution)/shard_map/gather | solution.py:63
  (71 shorter events, 29.8 us)
Async XLA Ops:
  0.6 246.0 %copy-start = (bf16[2,384,2048]{2,1,0:T(8,128)(2,1)S(1)}, bf16[2,384,2048]{2,1,0:T(8,128)(2,1)}, u32[]{:S(2)}) copy-start(bf16[2,384,2048]{2,1,0:T(8,128)(2,1)} %param.12) | copy-start | bytes 9437188
  3.1 0.8 copy-start.8
  29.7 10.5 %copy-start.12 = (f32[128,8]{0,1:T(8,128)S(1)}, f32[128,8]{0,1:T(8,128)}, u32[]{:S(2)}) copy-start(f32[128,8]{0,1:T(8,128)} %param.9) | copy-start | bytes 12292
  29.7 90.0 %all-to-all-start = ((bf16[64,24,2048]{2,1,0:T(8,128)(2,1)}), bf16[64,24,2048]{2,1,0:T(8,128)(2,1)}, u32[]{:S(2)}, u32[]{:S(2)}) async-start(bf16[64,24,2048]{2,1,0:T(8,128)(2,1)} %broadcast_select_fusion), calls=%async_computation | async-start | bytes 12582912 | tf_op jit(solution)/shard_map/all_to_all | solution.py:37
  40.4 6.0 %copy-start.2 = (bf16[128,1024]{1,0:T(8,128)(2,1)S(1)}, bf16[128,1024]{1,0:T(8,128)(2,1)}, u32[]{:S(2)}) copy-start(bf16[128,1024]{1,0:T(8,128)(2,1)} %param.13) | copy-start | bytes 786436
  125.2 97.3 %all-to-all-start.2 = ((bf16[128,24,1024]{2,1,0:T(8,128)(2,1)}), bf16[128,24,1024]{2,1,0:T(8,128)(2,1)}, u32[]{:S(2)}, u32[]{:S(2)}) async-start(bf16[128,24,1024]{2,1,0:T(8,128)(2,1)} %bitcast.142), calls=%async_computation.2 | async-start | bytes 12582912 | tf_op jit(solution)/shard_map/all_to_all | solution.py:50
  140.1 6.4 %copy-start.6 = (bf16[2,2048,384]{2,1,0:T(8,128)(2,1)S(1)}, bf16[2,2048,384]{2,1,0:T(8,128)(2,1)}, u32[]{:S(2)}) copy-start(bf16[2,2048,384]{2,1,0:T(8,128)(2,1)} %param.11) | copy-start | bytes 9437188
  146.5 4.8 copy-start.3
  146.5 4.8 copy-start.4
  256.4 1.0 copy-start.13
  286.1 7.3 %copy-start.5 = (bf16[2,2048,384]{2,1,0:T(8,128)(2,1)S(1)}, bf16[2,2048,384]{2,1,0:T(8,128)(2,1)}, u32[]{:S(2)}) copy-start(bf16[2,2048,384]{2,1,0:T(8,128)(2,1)} %param.10) | copy-start | bytes 9437188
  286.1 88.8 %all-to-all-start.1 = ((bf16[128,24,1024]{2,1,0:T(8,128)(2,1)}), bf16[128,24,1024]{2,1,0:T(8,128)(2,1)}, u32[]{:S(2)}, u32[]{:S(2)}) async-start(bf16[128,24,1024]{2,1,0:T(8,128)(2,1)} %bitcast.143), calls=%async_computation.1 | async-start | bytes 12582912 | tf_op jit(solution)/shard_map/all_to_all | solution.py:60
  392.1 4.8 copy-start.7
  392.1 4.8 copy-start.10
  396.8 8.4 %collective-permute-start = (f32[128,8]{1,0:T(8,128)S(1)}, f32[128,8]{1,0:T(8,128)S(1)}, u32[]{:S(2)}, u32[]{:S(2)}) collective-permute-start(f32[128,8]{1,0:T(8,128)S(1)} %get-tuple-element.16), channel_id=1, source_target_pairs={{0,1},{1,0},{2,3},{3,2},{4,5},{5,4},{6,7},{7,6},{8,9},{9,8},{10,11... | collective-permute-start | bytes 12296 | tf_op jit(solution)/shard_map/ppermute | solution.py:93
  428.5 8.0 %copy-start.14 = (bf16[64,2,12,384]{3,0,2,1:T(8,128)(2,1)S(1)}, bf16[64,2,12,384]{3,0,2,1:T(8,128)(2,1)}, u32[]{:S(2)}) copy-start(bf16[64,2,12,384]{3,0,2,1:T(8,128)(2,1)} %copy-done.13) | copy-start | bytes 3538948
  428.5 90.3 %all-to-all-start.3 = ((bf16[128,24,1024]{2,1,0:T(8,128)(2,1)}), bf16[128,24,1024]{2,1,0:T(8,128)(2,1)}, u32[]{:S(2)}, u32[]{:S(2)}) async-start(bf16[128,24,1024]{2,1,0:T(8,128)(2,1)} %bitcast.141), calls=%async_computation.3 | async-start | bytes 12582912 | tf_op jit(solution)/shard_map/all_to_all | solution.py:60
  436.4 7.3 %copy-start.11 = (bf16[64,2,12,384]{3,0,2,1:T(8,128)(2,1)S(1)}, bf16[64,2,12,384]{3,0,2,1:T(8,128)(2,1)}, u32[]{:S(2)}) copy-start(bf16[64,2,12,384]{3,0,2,1:T(8,128)(2,1)} %get-tuple-element.20) | copy-start | bytes 3538948
  436.5 15.3 %slice-start = ((s8[6291456]{0:T(1024)(128)(4,1)}), s8[4194304]{0:T(1024)(128)(4,1)S(1)}, s32[]{:S(2)}) async-start(s8[6291456]{0:T(1024)(128)(4,1)} %bitcast.152), calls=%async_computation.4 | async-start | bytes 8388608
  443.7 8.1 %slice-start.1 = ((s8[6291456]{0:T(1024)(128)(4,1)}), s8[2097152]{0:T(1024)(128)(4,1)S(1)}, s32[]{:S(2)}) async-start(s8[6291456]{0:T(1024)(128)(4,1)} %bitcast.152), calls=%async_computation.5 | async-start | bytes 4194304
  443.7 8.1 %copy-start.9 = (bf16[64,2,12,384]{3,0,2,1:T(8,128)(2,1)S(1)}, bf16[64,2,12,384]{3,0,2,1:T(8,128)(2,1)}, u32[]{:S(2)}) copy-start(bf16[64,2,12,384]{3,0,2,1:T(8,128)(2,1)} %get-tuple-element.21) | copy-start | bytes 3538948
  526.8 13.3 %copy-start.1 = (bf16[2,384,2048]{2,1,0:T(8,128)(2,1)S(1)}, bf16[2,384,2048]{2,1,0:T(8,128)(2,1)}, u32[]{:S(2)}) copy-start(bf16[2,384,2048]{2,1,0:T(8,128)(2,1)} %param.12) | copy-start | bytes 9437188

commit v6 on v2

v6 whole, which is shorter than its diff:
```python
import jax
import jax.numpy as jnp
from jax import lax
from jax.sharding import PartitionSpec as P


def body(tokens, routes, probs, w_gate, w_up, w_down, cotangent):
    tok_count, width = tokens.shape
    top_count = routes.shape[1]
    owners = lax.axis_size("dp")
    cols = lax.axis_size("col")
    local_experts = w_gate.shape[0]
    experts = local_experts * owners
    slot_cap = 3 * tok_count * top_count // (2 * experts)
    half_width = width // cols
    pair_count = tok_count * top_count
    rows_per_owner = local_experts * slot_cap
    slots = experts * slot_cap

    flat_routes = routes.reshape(-1)
    expert_ids = jnp.arange(experts, dtype=jnp.int32)
    onehot = (flat_routes[:, None] == expert_ids[None, :]).astype(jnp.int32)
    before = jnp.cumsum(onehot, axis=0) - onehot
    slot_index = jnp.sum(before * onehot, axis=1)
    flat_index = flat_routes * slot_cap + slot_index

    slot_ids = jnp.arange(slots, dtype=jnp.int32)
    match = flat_index.reshape(tok_count, top_count)[:, :, None] == slot_ids[None, None, :]
    weight = jnp.sum(jnp.where(match, probs[:, :, None], 0.0), axis=1)
    taken = jnp.any(match, axis=1)
    picker = taken.astype(jnp.bfloat16)
    weight_hi = weight.astype(jnp.bfloat16)
    weight_lo = (weight - weight_hi.astype(jnp.float32)).astype(jnp.bfloat16)
    prob_of_slot = jnp.sum(weight, axis=0)

    both = ("dp", "col")

    col_me = lax.axis_index("col")
    cot_other = lax.ppermute(cotangent, "col", perm=[(0, 1), (1, 0)])
    cot_full = jnp.where(
        col_me == 0,
        jnp.concatenate([cotangent, cot_other], axis=1),
        jnp.concatenate([cot_other, cotangent], axis=1),
    )

    tok_rows = jnp.einsum("ts,td->sd", picker, tokens, preferred_element_type=jnp.float32)
    cot_rows = jnp.einsum("ts,td->sd", picker, cot_full, preferred_element_type=jnp.float32)
    send = jnp.concatenate(
        [tok_rows.astype(jnp.bfloat16), (prob_of_slot[:, None] * cot_rows).astype(jnp.bfloat16)],
        axis=1,
    )
    arrived = lax.all_to_all(
        send.reshape(owners, rows_per_owner, 2 * width), "dp", 0, 0, tiled=True
    )
    row_block = arrived[:, :, :width]
    d_out = arrived[:, :, width:]

    expert_of_row = jnp.arange(rows_per_owner, dtype=jnp.int32) // slot_cap
    own = (expert_of_row[:, None] == jnp.arange(local_experts, dtype=jnp.int32)[None, :])[
        None, :, :, None
    ]

    def per_half(table):
        return jnp.broadcast_to(
            table.reshape(tok_count, owners, 1, rows_per_owner),
            (tok_count, owners, cols, rows_per_owner),
        )

    def send_back(halves):
        part = jnp.stack([h.astype(jnp.bfloat16) for h in halves], axis=1)
        got = lax.all_to_all(
            part.reshape(owners * cols, rows_per_owner, half_width), both, 0, 0, tiled=True
        )
        return got.reshape(owners, cols, rows_per_owner, half_width)

    def combine(table, got):
        return jnp.einsum("tocr,ocrd->td", per_half(table), got, preferred_element_type=jnp.float32)

    def halves_of(ref, axis):
        return [lax.slice_in_dim(ref, j * half_width, (j + 1) * half_width, axis=axis) for j in range(cols)]

    gate_acts = jnp.einsum("srd,ldh->srlh", row_block, w_gate, preferred_element_type=jnp.float32)
    up_acts = jnp.einsum("srd,ldh->srlh", row_block, w_up, preferred_element_type=jnp.float32)
    gate_acts = jnp.where(own, gate_acts, 0.0)
    up_acts = jnp.where(own, up_acts, 0.0)
    sigmoid_g = jax.nn.sigmoid(gate_acts)
    silu_g = gate_acts * sigmoid_g
    hidden = (silu_g * up_acts).astype(jnp.bfloat16)
    got_out = send_back(
        [
            jnp.einsum("srlh,lhd->srd", hidden, w, preferred_element_type=jnp.float32)
            for w in halves_of(w_down, 2)
        ]
    )
    mixed = (combine(weight_hi, got_out) + combine(weight_lo, got_out)).astype(jnp.bfloat16)
    dots = jnp.einsum("td,ocrd->tocr", cotangent, got_out, preferred_element_type=jnp.float32)
    dots = jnp.sum(dots, axis=2).reshape(tok_count, 1, slots)
    prob_part = jnp.sum(jnp.where(match, dots, 0.0), axis=2)

    grad_down = jnp.einsum(
        "srlh,srd->lhd", hidden, d_out, preferred_element_type=jnp.float32
    ).astype(jnp.bfloat16)
    d_hidden = jnp.einsum("srd,lhd->srlh", d_out, w_down, preferred_element_type=jnp.float32)
    d_hidden = jnp.where(own, d_hidden, 0.0)
    d_gate = (d_hidden * up_acts * sigmoid_g * (1.0 + gate_acts * (1.0 - sigmoid_g))).astype(
        jnp.bfloat16
    )
    d_up = (d_hidden * silu_g).astype(jnp.bfloat16)
    grad_gate = jnp.einsum(
        "srd,srlh->ldh", row_block, d_gate, preferred_element_type=jnp.float32
    ).astype(jnp.bfloat16)
    grad_up = jnp.einsum(
        "srd,srlh->ldh", row_block, d_up, preferred_element_type=jnp.float32
    ).astype(jnp.bfloat16)
    got_grad = send_back(
        [
            jnp.einsum("srlh,ldh->srd", d_gate, wg, preferred_element_type=jnp.float32)
            + jnp.einsum("srlh,ldh->srd", d_up, wu, preferred_element_type=jnp.float32)
            for wg, wu in zip(halves_of(w_gate, 1), halves_of(w_up, 1))
        ]
    )
    grad_tokens = combine(picker, got_grad).astype(jnp.bfloat16)
    grad_probs = lax.psum(prob_part, "col")
    return (mixed, grad_tokens, grad_probs, grad_gate, grad_up, grad_down)


def solution(mesh):
    return jax.shard_map(
        body,
        mesh=mesh,
        in_specs=(
            P("dp", None),
            P("dp", None),
            P("dp", None),
            P("dp", None, "col"),
            P("dp", None, "col"),
            P("dp", "col", None),
            P("dp", "col"),
        ),
        out_specs=(
            P("dp", "col"),
            P("dp", "col"),
            P("dp", None),
            P("dp", None, "col"),
            P("dp", None, "col"),
            P("dp", "col", None),
        ),
        check_vma=False,
    )
```

time: 521 us -> 489 us (0.939)
  blocking collectives: 163 us -> 68.5 us
  waiting for transfers between devices: 140 us -> 219 us
  local copies, waits for them, and re-layouts: 84.1 us -> 22.2 us
  matrix products: 94.3 us -> 121 us
  starting transfers between devices: 21.6 us -> 32 us
  other arithmetic: 9.87 us -> 17.1 us
    all_to_all x2 -> x0, blocking collectives: 163 us -> none  [the longest x1 82.8 us: body(): lax.all_to_all(send_tok.reshape(owners, rows_per_owner, width), 'dp', 0,...]
    all_to_all x2 -> x3, waiting for transfers between devices: 80.8 us -> 219 us  [the longest x1 172 us: body(): lax.all_to_all(send.reshape(owners, rows_per_owner, 2 * width), 'dp', 0,...]
    psum x0 -> x1, blocking collectives: none -> 68.5 us  [body(): grad_probs = lax.psum(prob_part, 'col')]
    ppermute x1, waiting for transfers between devices: 59.1 us -> 0.01 us  [body(): cot_other = lax.ppermute(cotangent, 'col', perm=[(0, 1), (1, 0)])]
    reshape x4 -> x0, local copies, waits for them, and re-layouts: 47.6 us -> none  [the longest x2 22.8 us: send_back(): partial_value.astype(jnp.bfloat16)]
    dot_general x10 -> x13, matrix products: 54.1 us -> 82.9 us  [the longest x1 14 us: body(): jnp.einsum('srd,lhd->srlh', d_out, w_down, preferred_element_type=jnp.flo...]
    transpose x2 -> x0, local copies, waits for them, and re-layouts: 24.2 us -> none  [send_back(): part.transpose(0, 2, 1, 3)]
    all_to_all x2 -> x3, starting transfers between devices: 20.2 us -> 30.6 us  [the longest x2 19.2 us: send_back(): lax.all_to_all(part.reshape(owners * cols, rows_per_owner, half_width), b...]
  transfers between devices with their start and end apart: 3 -> 4, of which waited for: 2 -> 2; matrix products, arithmetic and copies ran while one was open for 8% -> 17% of each run, Pallas kernels for 0% -> 0%
where the time goes in v6:
time: 489 us; the launch traced here: 481 us
  waiting for transfers between devices  219 us (45%)
  matrix products  121 us (25%)
  blocking collectives  68.5 us (14%)
  starting transfers between devices  32 us (7%)
  local copies, waits for them, and re-layouts  22.2 us (5%)
  other arithmetic  17.1 us (3%)
    all_to_all x1, waiting for transfers between devices, body(): lax.all_to_all(send.reshape(owners, rows_per_owner, 2 * width), 'dp', 0,...  172 us
    psum x1, blocking collectives, body(): grad_probs = lax.psum(prob_part, 'col')  68.5 us
    all_to_all x2, waiting for transfers between devices, send_back(): lax.all_to_all(part.reshape(owners * cols, rows_per_owner, half_width), b...  46.7 us
    dot_general x3, matrix products, combine(): jnp.einsum('tocr,ocrd->td', per_half(table), got, preferred_element_type=...  31.1 us
    all_to_all x2, starting transfers between devices, send_back(): lax.all_to_all(part.reshape(owners * cols, rows_per_owner, half_width), b...  19.2 us
    dot_general x1, matrix products, body(): jnp.einsum('srd,lhd->srlh', d_out, w_down, preferred_element_type=jnp.flo...  14 us
    unnamed x37, local copies, waits for them, and re-layouts  11.6 us
    all_to_all x1, starting transfers between devices, body(): lax.all_to_all(send.reshape(owners, rows_per_owner, 2 * width), 'dp', 0,...  11.4 us
  transfers between devices with their start and end apart: 4, of which 2 were waited for; matrix products, arithmetic and copies ran while one was open for 17% of the time, Pallas kernels for 0%

profile of v6, /device:TPU:82, one launch (start us, length us, event | category | flops | bytes accessed | tf_op | source)
XLA Modules:
  0.0 480.7 jit_solution(104147899719746415)
XLA Ops:
  5.6 3.1 fusion.4
  8.8 1.8 convolution_convert_fusion
  10.6 2.5 select_reduce_fusion.1
  13.1 1.9 multiply_convert_fusion
  15.0 5.1 %pad_maximum_fusion = bf16[1536,4096]{1,0:T(8,128)(2,1)} fusion(bf16[1536,2048]{1,0:T(8,128)(2,1)S(1)} %multiply_convert_fusion, bf16[1536,2048]{1,0:T(8,128)(2,1)S(1)} %convolution_convert_fusion), kind=kLoop, calls=%fused_computation | loop fusion | flops 25165824 | bytes 25165824 | tf_op jit(solution)/shard_map/concatenate | solution.py:48
  20.1 11.4 %all-to-all-start = ((bf16[64,24,4096]{2,1,0:T(8,128)(2,1)}), bf16[64,24,4096]{2,1,0:T(8,128)(2,1)}, u32[]{:S(2)}, u32[]{:S(2)}) async-start(bf16[64,24,4096]{2,1,0:T(8,128)(2,1)} %bitcast.159), calls=%async_computation | async-start | bytes 25165824 | tf_op jit(solution)/shard_map/all_to_all | solution.py:52
  34.7 172.4 %all-to-all-done = bf16[64,24,4096]{2,1,0:T(8,128)(2,1)} async-done(((bf16[64,24,4096]{2,1,0:T(8,128)(2,1)}), bf16[64,24,4096]{2,1,0:T(8,128)(2,1)}, u32[]{:S(2)}, u32[]{:S(2)}) %all-to-all-start) | async-done | bytes 12582944 | tf_op jit(solution)/shard_map/all_to_all | solution.py:52
  207.1 8.3 %fusion.17 = f32[64,24,2,384]{3,1,2,0:T(8,128)S(1)} fusion(bf16[2,2048,384]{2,1,0:T(8,128)(2,1)} %param.11, bf16[64,24,4096]{2,1,0:T(8,128)(2,1)} %all-to-all-done), kind=kOutput, calls=%fused_computation.39 | convolution fusion | flops 4831838208 | bytes 14155776 | tf_op jit(solution)/shard_map/srd,ldh->srlh/dot_general | solution.py:83
  215.4 8.8 %fusion.19 = f32[64,24,2,384]{3,1,2,0:T(8,128)} fusion(bf16[2,2048,384]{2,1,0:T(8,128)(2,1)S(1)} %copy-done.10, bf16[64,24,4096]{2,1,0:T(8,128)(2,1)} %all-to-all-done), kind=kOutput, calls=%fused_computation.41 | convolution fusion | flops 4831838208 | bytes 14155776 | tf_op jit(solution)/shard_map/srd,ldh->srlh/dot_general | solution.py:82
  224.2 14.0 %multiply_convert_fusion.1 = (bf16[64,24,2,384]{3,1,2,0:T(8,128)(2,1)S(1)}, bf16[64,24,2,384]{3,1,2,0:T(8,128)(2,1)}, bf16[64,24,2,384]{3,1,2,0:T(8,128)(2,1)S(1)}) fusion(pred[24,2]{0,1:T(4,128)(4,1)S(1)} %iota_compare_fusion.4, f32[64,24,2,384]{3,1,2,0:T(8,128)} %fusion.19, f32[64,24,2,384]{3,1,2,0:T(8,128)S(1)} %fusion.17, ...), kind=kOutput, calls=%fused_computation.29 | convolution fusion | flops 4853071872 | bytes 25952304 | tf_op jit(solution)/shard_map/srd,lhd->srlh/dot_general | solution.py:103
  238.3 4.0 fusion.13
  242.3 4.0 fusion.12
  246.3 9.3 %fusion.22 = bf16[2,2048,384]{1,2,0:T(8,128)(2,1)} fusion(bf16[64,24,2,384]{3,1,2,0:T(8,128)(2,1)S(1)} %get-tuple-element.34, bf16[64,24,4096]{2,1,0:T(8,128)(2,1)} %all-to-all-done), kind=kOutput, calls=%fused_computation.44 | convolution fusion | flops 4833411072 | bytes 11796480 | tf_op jit(solution)/shard_map/srd,srlh->ldh/dot_general | solution.py:112
  255.5 4.6 copy.89
  260.2 3.4 pad_maximum_fusion.1
  263.6 3.3 copy.78
  266.9 9.0 %all-to-all-start.1 = ((bf16[128,24,1024]{2,1,0:T(8,128)(2,1)}), bf16[128,24,1024]{2,1,0:T(8,128)(2,1)}, u32[]{:S(2)}, u32[]{:S(2)}) async-start(bf16[128,24,1024]{2,1,0:T(8,128)(2,1)} %bitcast.161), calls=%async_computation.1 | async-start | bytes 12582912 | tf_op jit(solution)/shard_map/all_to_all | solution.py:71
  275.9 9.4 %fusion.21 = bf16[2,2048,384]{1,2,0:T(8,128)(2,1)} fusion(bf16[64,24,2,384]{3,1,2,0:T(8,128)(2,1)} %get-tuple-element.35, bf16[64,24,4096]{2,1,0:T(8,128)(2,1)} %all-to-all-done), kind=kOutput, calls=%fused_computation.43 | convolution fusion | flops 4833411072 | bytes 11796480 | tf_op jit(solution)/shard_map/srd,srlh->ldh/dot_general | solution.py:109
  285.3 4.6 copy.88
  289.9 5.0 %fusion.24 = f32[64,24,1024,1]{2,1,3,0:T(8,128)S(1)} fusion(bf16[64,24,2,384]{3,1,2,0:T(8,128)(2,1)} %get-tuple-element.35, bf16[2,2048,384]{2,1,0:T(8,128)(2,1)} %param.10), kind=kOutput, calls=%fused_computation.46 | convolution fusion | flops 2415919104 | bytes 10223616 | tf_op jit(solution)/shard_map/srlh,ldh->srd/dot_general | solution.py:117
  294.9 2.7 fusion.27
  297.6 3.1 fusion.15
  300.8 3.1 fusion.14
  304.5 3.4 copy.84
  308.0 46.7 %all-to-all-done.1 = bf16[128,24,1024]{2,1,0:T(8,128)(2,1)} async-done(((bf16[128,24,1024]{2,1,0:T(8,128)(2,1)}), bf16[128,24,1024]{2,1,0:T(8,128)(2,1)}, u32[]{:S(2)}, u32[]{:S(2)}) %all-to-all-start.1) | async-done | bytes 6291488 | tf_op jit(solution)/shard_map/all_to_all | solution.py:71
  354.7 10.2 %all-to-all-start.2 = ((bf16[128,24,1024]{2,1,0:T(8,128)(2,1)}), bf16[128,24,1024]{2,1,0:T(8,128)(2,1)}, u32[]{:S(2)}, u32[]{:S(2)}) async-start(bf16[128,24,1024]{2,1,0:T(8,128)(2,1)} %bitcast.160), calls=%async_computation.2 | async-start | bytes 12582912 | tf_op jit(solution)/shard_map/all_to_all | solution.py:71
  365.0 9.3 %bitcast_convert_fusion = bf16[2,384,2048]{2,1,0:T(8,128)(2,1)} fusion(bf16[64,24,2,384]{3,1,2,0:T(8,128)(2,1)S(1)} %copy-done.15, bf16[64,24,4096]{2,1,0:T(8,128)(2,1)} %all-to-all-done), kind=kOutput, calls=%fused_computation.9 | convolution fusion | flops 4833411072 | bytes 11796480 | tf_op jit(solution)/shard_map/srlh,srd->lhd/dot_general | solution.py:100
  374.3 4.7 convolution_reduce_fusion
  380.2 68.5 %psum.7 = f32[128,8]{1,0:T(8,128)S(1)} all-reduce(f32[128,8]{1,0:T(8,128)S(1)} %select_reduce_fusion.2), channel_id=1, replica_groups=mesh['dp'=64,'col'=2] {'col'}, use_global_device_ids=true, to_apply=%region_8.9 | all-reduce | flops 1024 | bytes 8192 | tf_op jit(solution)/shard_map/psum | solution.py:123
  449.4 9.8 %fusion.37 = f32[128,1024]{1,0:T(8,128)S(1)} fusion(bf16[64,2,24,1024]{3,2,1,0:T(8,128)(2,1)} %bitcast.19, bf16[128,64,24]{0,1,2:T(8,128)(2,1)S(1)} %copy-done.6), kind=kOutput, calls=%fused_computation.60 | convolution fusion | flops 805306368 | bytes 7208960 | tf_op jit(solution)/shard_map/tocr,ocrd->td/dot_general | solution.py:77
  459.3 10.8 %fusion.49 = bf16[128,1024]{1,0:T(8,128)(2,1)} fusion(f32[128,1024]{1,0:T(8,128)S(1)} %fusion.37, bf16[64,2,24,1024]{3,2,1,0:T(8,128)(2,1)} %bitcast.19, bf16[128,64,24]{0,1,2:T(8,128)(2,1)S(1)} %copy-done.5), kind=kOutput, calls=%fused_computation.64 | convolution fusion | flops 805568512 | bytes 7471104 | tf_op jit(solution)/shard_map/tocr,ocrd->td/dot_general | solution.py:77
  470.0 10.5 %fusion.52 = bf16[128,1024]{1,0:T(8,128)(2,1)} fusion(bf16[64,2,24,1024]{3,2,1,0:T(8,128)(2,1)} %bitcast.43, bf16[128,64,24]{0,1,2:T(8,128)(2,1)S(1)} %copy-done.4), kind=kOutput, calls=%fused_computation.65 | convolution fusion | flops 805437440 | bytes 6946816 | tf_op jit(solution)/shard_map/tocr,ocrd->td/dot_general | solution.py:77
  (64 shorter events, 10.6 us)
Async XLA Ops:
  0.6 8.1 %copy-start = (bf16[128,2048]{1,0:T(8,128)(2,1)S(1)}, bf16[128,2048]{1,0:T(8,128)(2,1)}, u32[]{:S(2)}) copy-start(bf16[128,2048]{1,0:T(8,128)(2,1)} %param.7) | copy-start | bytes 1572868
  0.6 12.5 %collective-permute-start = (bf16[128,1024]{1,0:T(8,128)(2,1)}, bf16[128,1024]{1,0:T(8,128)(2,1)S(1)}, u32[]{:S(2)}, u32[]{:S(2)}) collective-permute-start(bf16[128,1024]{1,0:T(8,128)(2,1)} %param.13), channel_id=1, source_target_pairs={{0,1},{1,0},{2,3},{3,2},{4,5},{5,4},{6,7},{7,6},{8,9},{9,8},{10,11... | collective-permute-start | bytes 786440 | tf_op jit(solution)/shard_map/ppermute | solution.py:39
  5.6 5.0 %copy-start.2 = (s32[128,8]{1,0:T(8,128)}, s32[128,8]{1,0:T(8,128)S(1)}, u32[]{:S(2)}) copy-start(s32[128,8]{1,0:T(8,128)S(1)} %copy.74) | copy-start | bytes 12292
  8.8 4.3 copy-start.7
  20.1 187.0 %all-to-all-start = ((bf16[64,24,4096]{2,1,0:T(8,128)(2,1)}), bf16[64,24,4096]{2,1,0:T(8,128)(2,1)}, u32[]{:S(2)}, u32[]{:S(2)}) async-start(bf16[64,24,4096]{2,1,0:T(8,128)(2,1)} %bitcast.159), calls=%async_computation | async-start | bytes 25165824 | tf_op jit(solution)/shard_map/all_to_all | solution.py:52
  207.1 8.3 %copy-start.10 = (bf16[2,2048,384]{2,1,0:T(8,128)(2,1)S(1)}, bf16[2,2048,384]{2,1,0:T(8,128)(2,1)}, u32[]{:S(2)}) copy-start(bf16[2,2048,384]{2,1,0:T(8,128)(2,1)} %param.10) | copy-start | bytes 9437188
  215.4 8.8 %copy-start.9 = (bf16[2,384,2048]{2,1,0:T(8,128)(2,1)S(1)}, bf16[2,384,2048]{2,1,0:T(8,128)(2,1)}, u32[]{:S(2)}) copy-start(bf16[2,384,2048]{2,1,0:T(8,128)(2,1)} %param.12) | copy-start | bytes 9437188
  238.3 4.0 copy-start.14
  266.9 87.8 %all-to-all-start.1 = ((bf16[128,24,1024]{2,1,0:T(8,128)(2,1)}), bf16[128,24,1024]{2,1,0:T(8,128)(2,1)}, u32[]{:S(2)}, u32[]{:S(2)}) async-start(bf16[128,24,1024]{2,1,0:T(8,128)(2,1)} %bitcast.161), calls=%async_computation.1 | async-start | bytes 12582912 | tf_op jit(solution)/shard_map/all_to_all | solution.py:71
  289.9 5.0 %copy-start.11 = (bf16[2,2048,384]{2,1,0:T(8,128)(2,1)S(1)}, bf16[2,2048,384]{2,1,0:T(8,128)(2,1)}, u32[]{:S(2)}) copy-start(bf16[2,2048,384]{2,1,0:T(8,128)(2,1)} %param.10) | copy-start | bytes 9437188
  289.9 5.0 %copy-start.13 = (bf16[64,24,2,384]{3,1,2,0:T(8,128)(2,1)S(1)}, bf16[64,24,2,384]{3,1,2,0:T(8,128)(2,1)}, u32[]{:S(2)}) copy-start(bf16[64,24,2,384]{3,1,2,0:T(8,128)(2,1)} %get-tuple-element.35) | copy-start | bytes 7077892
  294.9 2.7 copy-start.12
  354.7 10.3 %copy-start.15 = (bf16[64,24,2,384]{3,1,2,0:T(8,128)(2,1)S(1)}, bf16[64,24,2,384]{3,1,2,0:T(8,128)(2,1)}, u32[]{:S(2)}) copy-start(bf16[64,24,2,384]{3,1,2,0:T(8,128)(2,1)} %copy-done.14) | copy-start | bytes 7077892
  354.7 115.3 %all-to-all-start.2 = ((bf16[128,24,1024]{2,1,0:T(8,128)(2,1)}), bf16[128,24,1024]{2,1,0:T(8,128)(2,1)}, u32[]{:S(2)}, u32[]{:S(2)}) async-start(bf16[128,24,1024]{2,1,0:T(8,128)(2,1)} %bitcast.160), calls=%async_computation.2 | async-start | bytes 12582912 | tf_op jit(solution)/shard_map/all_to_all | solution.py:71
  364.9 9.3 %copy-start.8 = (bf16[128,1024]{1,0:T(8,128)(2,1)S(1)}, bf16[128,1024]{1,0:T(8,128)(2,1)}, u32[]{:S(2)}) copy-start(bf16[128,1024]{1,0:T(8,128)(2,1)} %param.13) | copy-start | bytes 786436
  374.3 5.0 %copy-start.3 = (s32[128,8]{1,0:T(8,128)S(1)}, s32[128,8]{1,0:T(8,128)}, u32[]{:S(2)}) copy-start(s32[128,8]{1,0:T(8,128)} %copy-done.2) | copy-start | bytes 12292
  374.3 75.1 %copy-start.6 = (bf16[128,64,24]{0,1,2:T(8,128)(2,1)S(1)}, bf16[128,64,24]{0,1,2:T(8,128)(2,1)}, u32[]{:S(2)}) copy-start(bf16[128,64,24]{0,1,2:T(8,128)(2,1)} %copy.77) | copy-start | bytes 1179652
  379.3 79.9 %copy-start.5 = (bf16[128,64,24]{0,1,2:T(8,128)(2,1)S(1)}, bf16[128,64,24]{0,1,2:T(8,128)(2,1)}, u32[]{:S(2)}) copy-start(bf16[128,64,24]{0,1,2:T(8,128)(2,1)} %copy.80) | copy-start | bytes 1179652
  459.2 10.8 %copy-start.4 = (bf16[128,64,24]{0,1,2:T(8,128)(2,1)S(1)}, bf16[128,64,24]{0,1,2:T(8,128)(2,1)}, u32[]{:S(2)}) copy-start(bf16[128,64,24]{0,1,2:T(8,128)(2,1)} %copy.83) | copy-start | bytes 1179652
  459.2 21.3 %copy-start.1 = (bf16[128,2048]{1,0:T(8,128)(2,1)S(1)}, bf16[128,2048]{1,0:T(8,128)(2,1)}, u32[]{:S(2)}) copy-start(bf16[128,2048]{1,0:T(8,128)(2,1)} %param.7) | copy-start | bytes 1572868

commit v7 on v6

--- a/solution.py
+++ b/solution.py
@@ -92,7 +92,12 @@
             for w in halves_of(w_down, 2)
         ]
     )
-    mixed = (combine(weight_hi, got_out) + combine(weight_lo, got_out)).astype(jnp.bfloat16)
+    stacked = jnp.broadcast_to(
+        jnp.stack([weight_hi, weight_lo]).reshape(2, tok_count, owners, 1, rows_per_owner),
+        (2, tok_count, owners, cols, rows_per_owner),
+    )
+    both_parts = jnp.einsum("utocr,ocrd->utd", stacked, got_out, preferred_element_type=jnp.float32)
+    mixed = (both_parts[0] + both_parts[1]).astype(jnp.bfloat16)
     dots = jnp.einsum("td,ocrd->tocr", cotangent, got_out, preferred_element_type=jnp.float32)
     dots = jnp.sum(dots, axis=2).reshape(tok_count, 1, slots)
     prob_part = jnp.sum(jnp.where(match, dots, 0.0), axis=2)
@@ -120,6 +125,7 @@
         ]
     )
     grad_tokens = combine(picker, got_grad).astype(jnp.bfloat16)
+    prob_part, mixed = lax.optimization_barrier((prob_part, mixed))
     grad_probs = lax.psum(prob_part, "col")
     return (mixed, grad_tokens, grad_probs, grad_gate, grad_up, grad_down)
 

time: 489 us -> 476 us (0.973)
  matrix products: 121 us -> 110 us
  blocking collectives: 68.5 us -> 57.7 us
  starting transfers between devices: 32 us -> 39.8 us
    dot_general x3 -> x1, matrix products: 31.1 us -> 10.5 us  [combine(): jnp.einsum('tocr,ocrd->td', per_half(table), got, preferred_element_type=...]
    psum x1, blocking collectives: 68.5 us -> 57.7 us  [body(): grad_probs = lax.psum(prob_part, 'col')]
    dot_general x0 -> x1, matrix products: none -> 10.1 us  [body(): jnp.einsum('utocr,ocrd->utd', stacked, got_out, preferred_element_type=jn...]
    all_to_all x2, starting transfers between devices: 19.2 us -> 27.3 us  [send_back(): lax.all_to_all(part.reshape(owners * cols, rows_per_owner, half_width), b...]
    unnamed x37 -> x35, local copies, waits for them, and re-layouts: 11.6 us -> 11.6 us
  transfers between devices with their start and end apart: 4 -> 4, of which waited for: 2 -> 2; matrix products, arithmetic and copies ran while one was open for 17% -> 15% of each run, Pallas kernels for 0% -> 0%
where the time goes in v7:
time: 476 us; the launch traced here: 468 us
  waiting for transfers between devices  220 us (46%)
  matrix products  110 us (23%)
  blocking collectives  57.7 us (12%)
  starting transfers between devices  39.8 us (8%)
  local copies, waits for them, and re-layouts  21.6 us (5%)
  other arithmetic  18 us (4%)
    all_to_all x1, waiting for transfers between devices, body(): lax.all_to_all(send.reshape(owners, rows_per_owner, 2 * width), 'dp', 0,...  173 us
    psum x1, blocking collectives, body(): grad_probs = lax.psum(prob_part, 'col')  57.7 us
    all_to_all x2, waiting for transfers between devices, send_back(): lax.all_to_all(part.reshape(owners * cols, rows_per_owner, half_width), b...  46.7 us
    all_to_all x2, starting transfers between devices, send_back(): lax.all_to_all(part.reshape(owners * cols, rows_per_owner, half_width), b...  27.3 us
    dot_general x1, matrix products, body(): jnp.einsum('srd,lhd->srlh', d_out, w_down, preferred_element_type=jnp.flo...  14 us
    unnamed x35, local copies, waits for them, and re-layouts  11.6 us
    all_to_all x1, starting transfers between devices, body(): lax.all_to_all(send.reshape(owners, rows_per_owner, 2 * width), 'dp', 0,...  11.2 us
    dot_general x1, matrix products, combine(): jnp.einsum('tocr,ocrd->td', per_half(table), got, preferred_element_type=...  10.5 us
  transfers between devices with their start and end apart: 4, of which 2 were waited for; matrix products, arithmetic and copies ran while one was open for 15% of the time, Pallas kernels for 0%

profile of v7, /device:TPU:82, one launch (start us, length us, event | category | flops | bytes accessed | tf_op | source)
XLA Modules:
  0.0 468.2 jit_solution(7683592676164568193)
XLA Ops:
  0.6 1.4 collective-permute-start
  5.6 3.1 fusion.6
  8.8 1.8 convolution_convert_fusion
  10.6 2.5 select_reduce_fusion
  13.1 1.9 multiply_convert_fusion
  15.0 5.1 %pad_maximum_fusion = bf16[1536,4096]{1,0:T(8,128)(2,1)} fusion(bf16[1536,2048]{1,0:T(8,128)(2,1)S(1)} %multiply_convert_fusion, bf16[1536,2048]{1,0:T(8,128)(2,1)S(1)} %convolution_convert_fusion), kind=kLoop, calls=%fused_computation | loop fusion | flops 25165824 | bytes 25165824 | tf_op jit(solution)/shard_map/concatenate | solution.py:48
  20.1 11.2 %all-to-all-start = ((bf16[64,24,4096]{2,1,0:T(8,128)(2,1)}), bf16[64,24,4096]{2,1,0:T(8,128)(2,1)}, u32[]{:S(2)}, u32[]{:S(2)}) async-start(bf16[64,24,4096]{2,1,0:T(8,128)(2,1)} %bitcast.157), calls=%async_computation | async-start | bytes 25165824 | tf_op jit(solution)/shard_map/all_to_all | solution.py:52
  34.0 172.9 %all-to-all-done = bf16[64,24,4096]{2,1,0:T(8,128)(2,1)} async-done(((bf16[64,24,4096]{2,1,0:T(8,128)(2,1)}), bf16[64,24,4096]{2,1,0:T(8,128)(2,1)}, u32[]{:S(2)}, u32[]{:S(2)}) %all-to-all-start) | async-done | bytes 12582944 | tf_op jit(solution)/shard_map/all_to_all | solution.py:52
  206.9 8.3 %fusion.15 = f32[64,24,2,384]{3,1,2,0:T(8,128)S(1)} fusion(bf16[2,2048,384]{2,1,0:T(8,128)(2,1)} %param.11, bf16[64,24,4096]{2,1,0:T(8,128)(2,1)} %all-to-all-done), kind=kOutput, calls=%fused_computation.37 | convolution fusion | flops 4831838208 | bytes 14155776 | tf_op jit(solution)/shard_map/srd,ldh->srlh/dot_general | solution.py:83
  215.2 8.8 %fusion.17 = f32[64,24,2,384]{3,1,2,0:T(8,128)} fusion(bf16[2,2048,384]{2,1,0:T(8,128)(2,1)S(1)} %copy-done.9, bf16[64,24,4096]{2,1,0:T(8,128)(2,1)} %all-to-all-done), kind=kOutput, calls=%fused_computation.39 | convolution fusion | flops 4831838208 | bytes 14155776 | tf_op jit(solution)/shard_map/srd,ldh->srlh/dot_general | solution.py:82
  224.0 14.0 %multiply_convert_fusion.1 = (bf16[64,24,2,384]{3,1,2,0:T(8,128)(2,1)S(1)}, bf16[64,24,2,384]{3,1,2,0:T(8,128)(2,1)}, bf16[64,24,2,384]{3,1,2,0:T(8,128)(2,1)S(1)}) fusion(pred[24,2]{0,1:T(4,128)(4,1)S(1)} %iota_compare_fusion.4, f32[64,24,2,384]{3,1,2,0:T(8,128)} %fusion.17, f32[64,24,2,384]{3,1,2,0:T(8,128)S(1)} %fusion.15, ...), kind=kOutput, calls=%fused_computation.27 | convolution fusion | flops 4853071872 | bytes 25952304 | tf_op jit(solution)/shard_map/srd,lhd->srlh/dot_general | solution.py:108
  238.1 4.0 fusion.11
  242.1 4.0 fusion.10
  246.1 9.3 %fusion.20 = bf16[2,2048,384]{1,2,0:T(8,128)(2,1)} fusion(bf16[64,24,2,384]{3,1,2,0:T(8,128)(2,1)S(1)} %get-tuple-element.38, bf16[64,24,4096]{2,1,0:T(8,128)(2,1)} %all-to-all-done), kind=kOutput, calls=%fused_computation.42 | convolution fusion | flops 4833411072 | bytes 11796480 | tf_op jit(solution)/shard_map/srd,srlh->ldh/dot_general | solution.py:117
  255.3 4.6 copy.83
  260.0 3.4 pad_maximum_fusion.1
  263.4 3.3 copy.72
  266.7 17.2 %all-to-all-start.1 = ((bf16[128,24,1024]{2,1,0:T(8,128)(2,1)}), bf16[128,24,1024]{2,1,0:T(8,128)(2,1)}, u32[]{:S(2)}, u32[]{:S(2)}) async-start(bf16[128,24,1024]{2,1,0:T(8,128)(2,1)} %bitcast.159), calls=%async_computation.1 | async-start | bytes 12582912 | tf_op jit(solution)/shard_map/all_to_all | solution.py:71
  283.9 9.4 %fusion.19 = bf16[2,2048,384]{1,2,0:T(8,128)(2,1)} fusion(bf16[64,24,2,384]{3,1,2,0:T(8,128)(2,1)} %get-tuple-element.39, bf16[64,24,4096]{2,1,0:T(8,128)(2,1)} %all-to-all-done), kind=kOutput, calls=%fused_computation.41 | convolution fusion | flops 4833411072 | bytes 11796480 | tf_op jit(solution)/shard_map/srd,srlh->ldh/dot_general | solution.py:114
  293.3 4.6 copy.82
  298.0 5.0 %fusion.22 = f32[64,24,1024,1]{2,1,3,0:T(8,128)S(1)} fusion(bf16[64,24,2,384]{3,1,2,0:T(8,128)(2,1)} %get-tuple-element.39, bf16[2,2048,384]{2,1,0:T(8,128)(2,1)} %param.10), kind=kOutput, calls=%fused_computation.44 | convolution fusion | flops 2415919104 | bytes 10223616 | tf_op jit(solution)/shard_map/srlh,ldh->srd/dot_general | solution.py:122
  303.0 2.7 fusion.25
  305.7 3.1 fusion.13
  308.8 3.1 fusion.12
  312.6 3.4 copy.79
  316.0 46.7 %all-to-all-done.1 = bf16[128,24,1024]{2,1,0:T(8,128)(2,1)} async-done(((bf16[128,24,1024]{2,1,0:T(8,128)(2,1)}), bf16[128,24,1024]{2,1,0:T(8,128)(2,1)}, u32[]{:S(2)}, u32[]{:S(2)}) %all-to-all-start.1) | async-done | bytes 6291488 | tf_op jit(solution)/shard_map/all_to_all | solution.py:71
  362.7 10.0 %all-to-all-start.2 = ((bf16[128,24,1024]{2,1,0:T(8,128)(2,1)}), bf16[128,24,1024]{2,1,0:T(8,128)(2,1)}, u32[]{:S(2)}, u32[]{:S(2)}) async-start(bf16[128,24,1024]{2,1,0:T(8,128)(2,1)} %bitcast.158), calls=%async_computation.2 | async-start | bytes 12582912 | tf_op jit(solution)/shard_map/all_to_all | solution.py:71
  372.8 9.3 %bitcast_convert_fusion = bf16[2,384,2048]{2,1,0:T(8,128)(2,1)} fusion(bf16[64,24,2,384]{3,1,2,0:T(8,128)(2,1)S(1)} %copy-done.14, bf16[64,24,4096]{2,1,0:T(8,128)(2,1)} %all-to-all-done), kind=kOutput, calls=%fused_computation.9 | convolution fusion | flops 4833411072 | bytes 11796480 | tf_op jit(solution)/shard_map/srlh,srd->lhd/dot_general | solution.py:105
  382.1 4.7 %convolution_reduce_fusion = f32[64,24,128]{2,1,0:T(8,128)S(1)} fusion(bf16[64,2,24,1024]{3,2,1,0:T(8,128)(2,1)} %bitcast.18, bf16[128,1024]{1,0:T(8,128)(2,1)S(1)} %copy-done.7), kind=kOutput, calls=%fused_computation.57 | convolution fusion | flops 805502976 | bytes 7340032 | tf_op jit(solution)/shard_map/td,ocrd->tocr/dot_general | solution.py:101
  387.2 10.1 %fusion.35 = f32[2,128,1024]{2,1,0:T(8,128)S(1)} fusion(bf16[64,2,24,1024,1]{3,2,1,0,4:T(8,128)(2,1)} %bitcast.25, bf16[2,128,64,24]{1,2,3,0:T(8,128)(2,1)S(1)} %copy-done.4), kind=kOutput, calls=%fused_computation.58 | convolution fusion | flops 1610612736 | bytes 8126464 | tf_op jit(solution)/shard_map/utocr,ocrd->utd/dot_general | solution.py:99
  398.9 57.7 %psum.7 = f32[128,8]{1,0:T(8,128)S(1)} all-reduce(f32[128,8]{1,0:T(8,128)S(1)} %select_reduce_fusion.2), channel_id=1, replica_groups=mesh['dp'=64,'col'=2] {'col'}, use_global_device_ids=true, to_apply=%region_8.9 | all-reduce | flops 1024 | bytes 8192 | tf_op jit(solution)/shard_map/psum | solution.py:129
  457.3 10.5 %fusion.41 = bf16[128,1024]{1,0:T(8,128)(2,1)} fusion(bf16[64,2,24,1024]{3,2,1,0:T(8,128)(2,1)} %bitcast.49, bf16[128,64,24]{0,1,2:T(8,128)(2,1)S(1)} %copy-done.5), kind=kOutput, calls=%fused_computation.60 | convolution fusion | flops 805437440 | bytes 6946816 | tf_op jit(solution)/shard_map/tocr,ocrd->td/dot_general | solution.py:77
  (62 shorter events, 9.4 us)
Async XLA Ops:
  0.6 8.1 %copy-start = (bf16[128,2048]{1,0:T(8,128)(2,1)S(1)}, bf16[128,2048]{1,0:T(8,128)(2,1)}, u32[]{:S(2)}) copy-start(bf16[128,2048]{1,0:T(8,128)(2,1)} %param.7) | copy-start | bytes 1572868
  0.6 12.5 %collective-permute-start = (bf16[128,1024]{1,0:T(8,128)(2,1)}, bf16[128,1024]{1,0:T(8,128)(2,1)S(1)}, u32[]{:S(2)}, u32[]{:S(2)}) collective-permute-start(bf16[128,1024]{1,0:T(8,128)(2,1)} %param.13), channel_id=1, source_target_pairs={{0,1},{1,0},{2,3},{3,2},{4,5},{5,4},{6,7},{7,6},{8,9},{9,8},{10,11... | collective-permute-start | bytes 786440 | tf_op jit(solution)/shard_map/ppermute | solution.py:39
  5.6 5.0 %copy-start.2 = (s32[128,8]{1,0:T(8,128)}, s32[128,8]{1,0:T(8,128)S(1)}, u32[]{:S(2)}) copy-start(s32[128,8]{1,0:T(8,128)S(1)} %copy.70) | copy-start | bytes 12292
  8.8 4.3 copy-start.6
  20.1 186.8 %all-to-all-start = ((bf16[64,24,4096]{2,1,0:T(8,128)(2,1)}), bf16[64,24,4096]{2,1,0:T(8,128)(2,1)}, u32[]{:S(2)}, u32[]{:S(2)}) async-start(bf16[64,24,4096]{2,1,0:T(8,128)(2,1)} %bitcast.157), calls=%async_computation | async-start | bytes 25165824 | tf_op jit(solution)/shard_map/all_to_all | solution.py:52
  206.9 8.3 %copy-start.9 = (bf16[2,2048,384]{2,1,0:T(8,128)(2,1)S(1)}, bf16[2,2048,384]{2,1,0:T(8,128)(2,1)}, u32[]{:S(2)}) copy-start(bf16[2,2048,384]{2,1,0:T(8,128)(2,1)} %param.10) | copy-start | bytes 9437188
  215.2 8.8 %copy-start.8 = (bf16[2,384,2048]{2,1,0:T(8,128)(2,1)S(1)}, bf16[2,384,2048]{2,1,0:T(8,128)(2,1)}, u32[]{:S(2)}) copy-start(bf16[2,384,2048]{2,1,0:T(8,128)(2,1)} %param.12) | copy-start | bytes 9437188
  238.1 4.0 copy-start.13
  266.7 96.0 %all-to-all-start.1 = ((bf16[128,24,1024]{2,1,0:T(8,128)(2,1)}), bf16[128,24,1024]{2,1,0:T(8,128)(2,1)}, u32[]{:S(2)}, u32[]{:S(2)}) async-start(bf16[128,24,1024]{2,1,0:T(8,128)(2,1)} %bitcast.159), calls=%async_computation.1 | async-start | bytes 12582912 | tf_op jit(solution)/shard_map/all_to_all | solution.py:71
  298.0 5.0 %copy-start.10 = (bf16[2,2048,384]{2,1,0:T(8,128)(2,1)S(1)}, bf16[2,2048,384]{2,1,0:T(8,128)(2,1)}, u32[]{:S(2)}) copy-start(bf16[2,2048,384]{2,1,0:T(8,128)(2,1)} %param.10) | copy-start | bytes 9437188
  298.0 5.0 %copy-start.12 = (bf16[64,24,2,384]{3,1,2,0:T(8,128)(2,1)S(1)}, bf16[64,24,2,384]{3,1,2,0:T(8,128)(2,1)}, u32[]{:S(2)}) copy-start(bf16[64,24,2,384]{3,1,2,0:T(8,128)(2,1)} %get-tuple-element.39) | copy-start | bytes 7077892
  302.9 2.7 copy-start.11
  362.7 10.1 %copy-start.14 = (bf16[64,24,2,384]{3,1,2,0:T(8,128)(2,1)S(1)}, bf16[64,24,2,384]{3,1,2,0:T(8,128)(2,1)}, u32[]{:S(2)}) copy-start(bf16[64,24,2,384]{3,1,2,0:T(8,128)(2,1)} %copy-done.13) | copy-start | bytes 7077892
  362.7 94.5 %all-to-all-start.2 = ((bf16[128,24,1024]{2,1,0:T(8,128)(2,1)}), bf16[128,24,1024]{2,1,0:T(8,128)(2,1)}, u32[]{:S(2)}, u32[]{:S(2)}) async-start(bf16[128,24,1024]{2,1,0:T(8,128)(2,1)} %bitcast.158), calls=%async_computation.2 | async-start | bytes 12582912 | tf_op jit(solution)/shard_map/all_to_all | solution.py:71
  372.8 9.3 %copy-start.7 = (bf16[128,1024]{1,0:T(8,128)(2,1)S(1)}, bf16[128,1024]{1,0:T(8,128)(2,1)}, u32[]{:S(2)}) copy-start(bf16[128,1024]{1,0:T(8,128)(2,1)} %param.13) | copy-start | bytes 786436
  382.1 5.0 %copy-start.4 = (bf16[2,128,64,24]{1,2,3,0:T(8,128)(2,1)S(1)}, bf16[2,128,64,24]{1,2,3,0:T(8,128)(2,1)}, u32[]{:S(2)}) copy-start(bf16[2,128,64,24]{1,2,3,0:T(8,128)(2,1)} %copy.75) | copy-start | bytes 2359300
  387.2 10.9 %copy-start.3 = (s32[128,8]{1,0:T(8,128)S(1)}, s32[128,8]{1,0:T(8,128)}, u32[]{:S(2)}) copy-start(s32[128,8]{1,0:T(8,128)} %copy-done.2) | copy-start | bytes 12292
  387.2 70.1 %copy-start.5 = (bf16[128,64,24]{0,1,2:T(8,128)(2,1)S(1)}, bf16[128,64,24]{0,1,2:T(8,128)(2,1)}, u32[]{:S(2)}) copy-start(bf16[128,64,24]{0,1,2:T(8,128)(2,1)} %copy.78) | copy-start | bytes 1179652
  397.3 70.5 %copy-start.1 = (bf16[128,2048]{1,0:T(8,128)(2,1)S(1)}, bf16[128,2048]{1,0:T(8,128)(2,1)}, u32[]{:S(2)}) copy-start(bf16[128,2048]{1,0:T(8,128)(2,1)} %param.7) | copy-start | bytes 1572868
